TPU v7x, 32 devices: a whole 2x2x4 slice. The times are simulated.
32 devices in a mesh: groups: 2 (over x), visit: 16 (over z, y, core).
Axes of the slice: x: 2, y: 2, z: 4, core: 2. Of those that a mesh axis runs over, the one named last changes fastest.
Arguments:
- science: float32 [8192, 1024], P(('groups', 'visit')), parts along dimension 0, may hold values from -6 to 6
- template: bfloat16 [8192, 1024], P(('groups', 'visit')), parts along dimension 0, may hold values from -6 to 6
- owner_map: int32 [32], P('groups'), parts along dimension 0, may hold values from 0 to 15, as said below
- covering: int32 [32, 4], P(('groups', 'visit')), parts along dimension 0, may hold values from 0 to 15, as said below
- row_shift: int32 [32, 4], P(('groups', 'visit')), parts along dimension 0, may hold values from -128 to 128, as said below
- col_shift: int32 [32, 4], P(('groups', 'visit')), parts along dimension 0, may hold values from -256 to 256, as said below
- basis_cols: float32 [20, 21], replicated, may hold values from -1.25 to 1.25
- basis_rows: float32 [20, 21], replicated, may hold values from -1.25 to 1.25
- coeffs: float32 [8, 20], P('groups'), parts along dimension 0, may hold values from -1.25 to 1.25
- psf_kernel: float32 [9, 9], replicated, may hold values from 0 to 0.25
Outputs:
- difference: float32 [8192, 1024], P(('groups', 'visit')), parts along dimension 0
- detection: float32 [8192, 1024], P(('groups', 'visit')), parts along dimension 0
There are 2 independent parts, one for each index of `groups`. A program takes and returns all parts, laid end to end along the dimension named above; an argument that names none is the same for every part. Nothing has to cross between parts.
Inputs may be any that keep to these rules, and one draw needn't show every extreme that they name: owner_map is a permutation: every device stores exactly one template piece. `covering`: the 4 pieces listed for a row block are different; the first is the piece stored on that block's own device; every listed piece is stored on a device at most 3 positions away along the visit axis, and on some device exactly 3. `row_shift`: the first slot of every row block has shift 0; both ends of the range are reached. `col_shift`: the first slot of every row block has shift 0; both ends of the range are reached.
All inputs are finite; a program needn't handle non-finite values.
Results may differ from a plain program's by a relative error of at most 0.005.
Values may be sent and summed in bfloat16 or wider, within the bound.
No kernel may reach another device: no remote copies, remote signals or barrier semaphores. Data moves between devices by JAX's collectives and lax.ppermute only.
A program may use at most 64 MiB of HBM per device.

v0:
```python
import jax
import jax.numpy as jnp
from jax import lax
from jax.experimental import pallas as pl
from jax.experimental.pallas import tpu as pltpu
from jax.sharding import PartitionSpec as P


PIECES = 4
LANES = 128

BUFFER_OF = ((4, 5, 6, 0, 1, 2, 3), (6, 5, 1, 0, 3, 2, 4), (4, 2, 3, 0, 1, 5, 6), (3, 2, 1, 0, 6, 5, 4))


def cost(megabytes):
    return pl.CostEstimate(flops=0, transcendentals=0, bytes_accessed=megabytes * 2**20)


def relay_kernel(far, pair, out):
    residue = lax.rem(lax.axis_index("visit"), 4)
    passes_far = (residue == 1) | (residue == 2)

    @pl.when(passes_far)
    def _():
        out[...] = far[...]

    @pl.when(jnp.logical_not(passes_far))
    def _():
        out[...] = pair[...]


def place_of():
    devices = lax.axis_size("visit")
    return lax.rem(lax.rem(lax.axis_index("visit") + 1, devices), PIECES)


def gather_pieces(own):
    count = lax.axis_size("visit")

    def move(value, pairs):
        kept = [(i, j) for i, j in pairs if 0 <= j < count]
        return lax.ppermute(value, "visit", kept)

    pair = move(own, [(i, i ^ 2) for i in range(count)])
    far = move(own, [(i, i + 3 if i % 2 else i - 3) for i in range(count)])
    partner = move(own, [(i, i ^ 1) for i in range(count)])
    whole = pl.BlockSpec(memory_space=pltpu.VMEM)
    relay = pl.pallas_call(
        relay_kernel,
        out_shape=jax.ShapeDtypeStruct(own.shape, own.dtype),
        in_specs=[whole, whole],
        out_specs=whole,
        compiler_params=pltpu.CompilerParams(vmem_limit_bytes=4 * 2**20),
        cost_estimate=cost(1),
        name="relay",
    )(far, pair)
    targets = {0: 4, 1: 1, 2: -1, 3: -4}
    relayed = move(relay, [(i, i + targets[i % 4]) for i in range(count)])
    crossed = move(pair, [(i, i ^ 1) for i in range(count)])
    relayed_crossed = move(relayed, [(i, i ^ 1) for i in range(count)])
    return (own, partner, pair, crossed, far, relayed, relayed_crossed)


CHUNK = 16


def spread(piece, turn, target, first):
    rows, cols = piece.shape
    blocks = cols // LANES

    def body(step, carry):
        row = pl.multiple_of(step * CHUNK, CHUNK)
        for k in range(blocks):
            tile = piece[pl.ds(row, CHUNK), k * LANES : (k + 1) * LANES].astype(jnp.float32)
            if turn is not None:
                tile = pltpu.roll(tile, turn, 1)
            target[pl.ds(first + row * blocks + k, CHUNK, stride=blocks), :] = tile
        return carry

    lax.fori_loop(0, rows // CHUNK, body, 0, unroll=4)


def shift_of(rows, blocks, row_shift, col_shift, valid):
    most = rows // 2
    base = (most + 1) * blocks
    lane = lax.broadcasted_iota(jnp.int32, (blocks, LANES), 1)
    block = lax.broadcasted_iota(jnp.int32, (blocks, LANES), 0)
    back = -col_shift
    start = lax.shift_right_arithmetic(back, 7)
    left = back - start * LANES
    turn = lax.bitwise_and(LANES - left, LANES - 1)
    limit = jnp.where(valid, blocks, -2 * blocks)
    here = block + start
    masks = (
        (lane < LANES - left) & (here >= 0) & (here < limit),
        (lane >= LANES - left) & (here >= -1) & (here < limit - 1),
    )
    return base, turn, base - row_shift * blocks + start, masks


def clear_ends(moved, rows, blocks):
    pad = rows // 2 * blocks
    base = pad + blocks
    moved[blocks:base, :] = jnp.zeros((pad, LANES), jnp.float32)
    moved[base + rows * blocks : base + rows * blocks + pad, :] = jnp.zeros((pad, LANES), jnp.float32)


def add_moved(rows, blocks, read, moves, write):
    def body(step, carry):
        for i in range(8):
            row = step * 8 + i
            value = read(row)
            for moved, start, masks in moves:
                low = moved[pl.ds(start + row * blocks, blocks), :]
                high = moved[pl.ds(start + row * blocks + 1, blocks), :]
                value = value + jnp.where(masks[0], low, jnp.where(masks[1], high, 0.0))
            write(row, value)
        return carry

    lax.fori_loop(0, rows // 8, body, 0, unroll=4)


def slot_of(covering, owner_map, slot):
    position = lax.axis_index("visit")
    residue = lax.rem(position, 4)
    distance = owner_map[covering[0, slot]] - position
    buffer = jnp.int32(0)
    for place, row in enumerate(BUFFER_OF):
        for index, held in enumerate(row):
            here = (residue == place) & (distance == index - len(row) // 2)
            buffer = jnp.where(here, held, buffer)
    return buffer


def late_slot(covering, owner_map, row_shift, col_shift, buffer):
    valid, rows, cols = jnp.int32(0), jnp.int32(0), jnp.int32(0)
    for slot in range(1, covering.shape[1]):
        here = slot_of(covering, owner_map, slot) == buffer
        valid = jnp.where(here, 1, valid)
        rows = jnp.where(here, row_shift[0, slot], rows)
        cols = jnp.where(here, col_shift[0, slot], cols)
    return valid > 0, rows, cols


def near_kernel(covering, owner_map, row_shift, col_shift, own_piece, *refs):
    pieces, (out, recip), (own, moved) = refs[:4], refs[4:6], refs[6:]
    rows, cols = own_piece.shape
    blocks = cols // LANES
    slots = moved.shape[0]
    spread(own_piece, None, own, 0)
    moves = []
    for slot in range(slots):
        held = slot_of(covering, owner_map, slot + 1)
        base, turn, start, masks = shift_of(
            rows, blocks, row_shift[0, slot + 1], col_shift[0, slot + 1], held <= len(pieces)
        )
        clear_ends(moved.at[slot], rows, blocks)
        for index in range(len(pieces)):

            @pl.when(held == index + 1)
            def _():
                spread(pieces[index], turn, moved.at[slot], base)

        moves.append((moved.at[slot], start, masks))

    def read(row):
        return own[pl.ds(pl.multiple_of(row * blocks, blocks), blocks), :]

    def write(row, value):
        out[row] = value

    add_moved(rows, blocks, read, moves, write)
    column = lax.broadcasted_iota(jnp.int32, (blocks, LANES), 0) * LANES
    column = column + lax.broadcasted_iota(jnp.int32, (blocks, LANES), 1)
    covers = []
    for slot in range(slots):
        source = column - col_shift[0, slot + 1]
        covers.append(jnp.where((source >= 0) & (source < cols), 1.0, 0.0))

    def cover(step, carry):
        for i in range(8):
            row = step * 8 + i
            total = jnp.ones((blocks, LANES), jnp.float32)
            for slot in range(slots):
                source = row - row_shift[0, slot + 1]
                inside = ((source >= 0) & (source < rows)).astype(jnp.float32)
                total = total + covers[slot] * inside
            recip[row] = 1.0 / total
        return carry

    lax.fori_loop(0, rows // 8, cover, 0, unroll=4)


def relayed_kernel(covering, owner_map, row_shift, col_shift, partial, piece, out, moved):
    rows, blocks, _ = partial.shape
    valid, row_move, col_move = late_slot(covering, owner_map, row_shift, col_shift, 5)
    base, turn, start, masks = shift_of(rows, blocks, row_move, col_move, valid)

    @pl.when(valid)
    def _():
        clear_ends(moved, rows, blocks)
        spread(piece, turn, moved, base)

    def write(row, value):
        out[row] = value

    add_moved(rows, blocks, lambda row: partial[row], [(moved, start, masks)], write)


def canvas_kernel(
    covering, owner_map, row_shift, col_shift, partial, piece, recip, first_rows, last_rows, out, to_inner, to_outer, moved,
):
    rows, blocks, _ = partial.shape
    valid, row_move, col_move = late_slot(covering, owner_map, row_shift, col_shift, 6)
    base, turn, start, masks = shift_of(rows, blocks, row_move, col_move, valid)

    @pl.when(valid)
    def _():
        clear_ends(moved, rows, blocks)
        spread(piece, turn, moved, base)

    def write(row, value):
        out[row] = value * recip[row]

    add_moved(rows, blocks, lambda row: partial[row], [(moved, start, masks)], write)
    edge = to_inner.shape[0] - first_rows.shape[0]
    even = lax.rem(place_of(), 2) == 0
    for message, up in ((to_inner, even), (to_outer, jnp.logical_not(even))):

        @pl.when(up)
        def _():
            message[:edge] = out[:edge].astype(jnp.bfloat16)
            message[edge:] = first_rows[...]

        @pl.when(jnp.logical_not(up))
        def _():
            message[:edge] = out[rows - edge :].astype(jnp.bfloat16)
            message[edge:] = last_rows[...]


def bands_of(taps, bands):
    count, lanes = taps.shape
    half = lanes // 2
    lower = lax.broadcasted_iota(jnp.int32, (lanes, lanes), 1) < half
    zero = jnp.zeros((lanes, lanes), jnp.float32)

    def table(tap, shift):
        if not 0 <= tap < count:
            return zero
        spread = jnp.broadcast_to(taps[tap : tap + 1, :], (lanes, lanes))
        return pltpu.roll(spread, shift, 1, stride=1, stride_axis=0)

    for offset in range(2 * bands.shape[1]):
        at = slice((offset % 2) * lanes, (offset % 2 + 1) * lanes)
        for pair in range(2):
            plain = table(offset - 2 * pair, 0)
            turned = table(offset - 2 * pair - 1, half)
            to = slice(pair * lanes, (pair + 1) * lanes)
            bands[0, offset // 2, at, to] = jnp.where(lower, plain, turned).astype(bands.dtype)
            bands[1, offset // 2, at, to] = jnp.where(lower, turned, plain).astype(bands.dtype)


def prepare_kernel(model_taps, psf_taps, top, bottom, model_bands, psf_bands, first_rows, last_rows, mixed):
    bands_of(model_taps, model_bands)
    bands_of(psf_taps, psf_bands)
    rows, cols = top.shape
    blocks = cols // LANES
    count = first_rows.shape[0] // 2
    for block, out, first in ((top, first_rows, 0), (bottom, last_rows, rows - count)):
        for k in range(blocks):
            mixed[pl.ds(k, rows, stride=blocks), :] = block[:, k * LANES : (k + 1) * LANES]
        for row in range(count):
            value = mixed[(first + row) * blocks : (first + row + 1) * blocks, :]
            high = value.astype(jnp.bfloat16)
            out[row] = high
            out[count + row] = (value - high.astype(jnp.float32)).astype(jnp.bfloat16)


def pack_rows(source, count, packed):
    blocks = 8
    lane = lax.broadcasted_iota(jnp.int32, (blocks, LANES), 1)
    block = lax.broadcasted_iota(jnp.int32, (blocks, LANES), 0)
    inner = block > 0
    outer = block < blocks - 1

    def sides(x):
        at = blocks * (x + 1)
        here = source[at : at + blocks, :]
        before = source[at - 1 : at - 1 + blocks, :]
        after = source[at + 1 : at + 1 + blocks, :]
        return (
            jnp.where(lane < 96, here, jnp.where(inner, before, 0.0)),
            jnp.where(lane >= 32, here, jnp.where(outer, after, 0.0)),
        )

    for phase in range(4):
        last = sides(phase)
        for h in range(1, count // 4):
            now = sides(4 * h + phase)
            odd, p = (h - 1) % 2, (h - 1) // 2
            for side in range(2):
                tile = jnp.concatenate([last[side], now[side]], axis=0).astype(jnp.bfloat16)
                to = slice((phase % 2) * LANES, (phase % 2 + 1) * LANES)
                packed[odd, side, phase // 2, 16 * p : 16 * p + 16, to] = tile
            last = now


def product_of(packed, bands, side, groups):
    chunks = bands.shape[1]
    left = []
    for chunk in range(chunks):
        q, pair = chunk // 2, chunk % 2
        first = 16 * (q // 2)
        left.append(packed[q % 2, side, pair, first : first + 8 * groups, :])
    right = bands[side].reshape(chunks * 256, 256)
    return jnp.dot(jnp.concatenate(left, axis=1), right, preferred_element_type=jnp.float32)


def unfold(packed, bands, groups, target):
    low = product_of(packed, bands, 0, groups)
    high = product_of(packed, bands, 1, groups)
    lower = lax.broadcasted_iota(jnp.int32, (8, LANES), 1) < LANES // 2
    for g in range(groups):
        rows = slice(8 * g, 8 * g + 8)
        for pair in range(2):
            lanes = slice(pair * LANES, (pair + 1) * LANES)
            a, b = low[rows, lanes], high[rows, lanes]
            to = 8 * (4 * g + 2 * pair)
            target[to : to + 8, :] = jnp.where(lower, a, b)
            target[to + 8 : to + 16, :] = pltpu.roll(jnp.where(lower, b, a), LANES // 2, 1)


def difference_kernel(
    rim, psf_rim, canvas, inner_rows, outer_rows, science, bands, difference, rounded, square, extended, packed, model,
):
    rows, cols = science.shape
    blocks = cols // LANES
    edge = rim + psf_rim
    first = blocks

    def put(x, values):
        extended[first + x * blocks : first + (x + values.shape[0]) * blocks, :] = values.reshape(-1, LANES)

    place = place_of()
    odd = lax.rem(place, 2) == 1
    put(edge, canvas[...])
    for swapped in range(2):

        @pl.when(odd == (swapped == 1))
        def _():
            above, below = (outer_rows, inner_rows) if swapped else (inner_rows, outer_rows)
            put(0, above[:edge].astype(jnp.float32))
            put(edge + rows, below[:edge].astype(jnp.float32))

    pack_rows(extended, rows + 2 * edge, packed)
    unfold(packed, bands, (rows + 2 * psf_rim) // 4, model)

    def body(step, total):
        row = pl.multiple_of(step * 8, 8)
        for k in range(blocks):
            here = slice(k * LANES, (k + 1) * LANES)
            at = pl.ds((row + psf_rim) * blocks + k, 8, stride=blocks)
            inner = science[pl.ds(row, 8), here] - model[at, :]
            difference[pl.ds(row, 8), here] = inner
            rounded[pl.ds(first + (row + psf_rim) * blocks + k, 8, stride=blocks), :] = inner
            total = total + inner * inner
        return total

    total = lax.fori_loop(0, rows // 8, body, jnp.zeros((8, LANES), jnp.float32), unroll=2)
    square[...] = jnp.broadcast_to(jnp.sum(total), square.shape)
    for swapped in range(2):

        @pl.when(odd == (swapped == 1))
        def _():
            above, below = (outer_rows, inner_rows) if swapped else (inner_rows, outer_rows)
            for joined, rows_of, x in ((place > 0, above, 0), (place < PIECES - 1, below, psf_rim + rows)):
                value = rows_of[edge : edge + psf_rim].astype(jnp.float32)
                value = value + rows_of[edge + psf_rim : edge + 2 * psf_rim].astype(jnp.float32)
                value = value.reshape(-1, LANES) - model[x * blocks : (x + psf_rim) * blocks, :]
                to = slice(first + x * blocks, first + (x + psf_rim) * blocks)
                rounded[to, :] = jnp.where(joined, value, 0.0)


def response_kernel(rounded, bands, response, packed, mixed):
    rows, cols = response.shape
    blocks = cols // LANES
    pack_rows(rounded, rounded.shape[0] // blocks - 2, packed)
    unfold(packed, bands, rows // 4, mixed)
    for row in range(0, rows, 8):
        for k in range(blocks):
            response[row : row + 8, k * LANES : (k + 1) * LANES] = mixed[pl.ds(row * blocks + k, 8, stride=blocks), :]


def detection_kernel(count, response, *refs):
    total = refs[0][...]
    for ref in refs[1:-1]:
        total = total + ref[...]
    scale = 1.0 / jnp.sqrt(total[:1, :1] / count + 1e-06)
    refs[-1][...] = response[...] * scale


def tap_rows(taps, width):
    rim = taps.shape[1] // 2
    turned = jnp.flip(taps, axis=1)
    gap = jnp.zeros((taps.shape[0], width - taps.shape[1]), jnp.float32)
    return jnp.concatenate([turned[:, rim:], gap, turned[:, :rim]], axis=1)


def shards(
    science,
    template,
    owner_map,
    covering,
    row_shift,
    col_shift,
    basis_cols,
    basis_rows,
    coeffs,
    psf_kernel,
):
    image_rows, image_cols = science.shape
    devices = lax.axis_size("visit")
    position = lax.axis_index("visit")
    held_piece = (position + 1) % devices
    visit_id = held_piece // PIECES
    slot_count = covering.shape[1]
    rim = basis_cols.shape[1] // 2
    psf_rim = psf_kernel.shape[0] // 2
    blocks = image_cols // LANES
    vmem = pl.BlockSpec(memory_space=pltpu.VMEM)
    smem = pl.BlockSpec(memory_space=pltpu.SMEM)

    pieces = gather_pieces(template)

    slot_args = (covering, owner_map, row_shift, col_shift)
    coeff_row = lax.dynamic_index_in_dim(coeffs, visit_id, 0, keepdims=False)
    weights = (coeff_row[:, None] * basis_rows).astype(jnp.bfloat16)
    model_taps = jnp.einsum(
        "bs,bt->st", weights, basis_cols.astype(jnp.bfloat16), preferred_element_type=jnp.float32
    )
    psf_taps = psf_kernel.astype(jnp.bfloat16).astype(jnp.float32)
    model_chunks = (basis_rows.shape[1] + 3) // 2
    psf_chunks = (psf_kernel.shape[0] + 3) // 2
    edge = rim + psf_rim
    sent = jax.ShapeDtypeStruct((edge + 2 * psf_rim, blocks, LANES), jnp.bfloat16)
    rim_rows = jax.ShapeDtypeStruct((2 * psf_rim, blocks, LANES), jnp.bfloat16)
    last_block = image_rows // 8 - 1
    model_bands, psf_bands, first_rows, last_rows = pl.pallas_call(
        prepare_kernel,
        out_shape=(
            jax.ShapeDtypeStruct((2, model_chunks, 256, 256), jnp.bfloat16),
            jax.ShapeDtypeStruct((2, psf_chunks, 256, 256), jnp.bfloat16),
            rim_rows,
            rim_rows,
        ),
        grid=(1,),
        in_specs=[
            vmem,
            vmem,
            pl.BlockSpec((8, image_cols), lambda i: (0, 0)),
            pl.BlockSpec((8, image_cols), lambda i: (last_block, 0)),
        ],
        out_specs=(vmem, vmem, vmem, vmem),
        scratch_shapes=[pltpu.VMEM((8 * blocks, LANES), jnp.float32)],
        compiler_params=pltpu.CompilerParams(vmem_limit_bytes=16 * 2**20),
        cost_estimate=cost(4),
        name="prepare",
    )(tap_rows(model_taps, LANES), tap_rows(psf_taps, LANES), science, science)

    moved_rows = (2 * image_rows + 3) * blocks
    canvas_shape = jax.ShapeDtypeStruct((image_rows, blocks, LANES), jnp.float32)
    moved = pltpu.VMEM((moved_rows, LANES), jnp.float32)
    partial, recip = pl.pallas_call(
        near_kernel,
        out_shape=(canvas_shape, canvas_shape),
        in_specs=[smem] * 4 + [vmem] * 5,
        out_specs=(vmem, vmem),
        scratch_shapes=[
            pltpu.VMEM((image_rows * blocks, LANES), jnp.float32),
            pltpu.VMEM((slot_count - 1, moved_rows, LANES), jnp.float32),
        ],
        compiler_params=pltpu.CompilerParams(vmem_limit_bytes=20 * 2**20),
        cost_estimate=cost(11),
        name="near",
    )(*slot_args, *pieces[:5])
    partial = pl.pallas_call(
        relayed_kernel,
        out_shape=canvas_shape,
        in_specs=[smem] * 4 + [vmem] * 2,
        out_specs=vmem,
        scratch_shapes=[moved],
        compiler_params=pltpu.CompilerParams(vmem_limit_bytes=12 * 2**20),
        cost_estimate=cost(5),
        name="relayed",
    )(*slot_args, partial, pieces[5])
    canvas, to_inner, to_outer = pl.pallas_call(
        canvas_kernel,
        out_shape=(canvas_shape, sent, sent),
        in_specs=[smem] * 4 + [vmem] * 5,
        out_specs=(vmem, vmem, vmem),
        scratch_shapes=[moved],
        compiler_params=pltpu.CompilerParams(vmem_limit_bytes=12 * 2**20),
        cost_estimate=cost(5),
        name="canvas",
    )(*slot_args, partial, pieces[6], recip, first_rows, last_rows)

    groups = [[(first + i - 1) % devices for i in range(PIECES)] for first in range(0, devices, PIECES)]

    def swap(value, pairs):
        return lax.ppermute(value, "visit", [(g[a], g[b]) for g in groups for a, b in pairs])

    inner_rows = swap(to_inner, [(1, 2), (2, 1)])
    outer_rows = swap(to_outer, [(0, 1), (1, 0), (2, 3), (3, 2)])

    rounded_rows = image_rows + 2 * psf_rim
    difference, rounded, square = pl.pallas_call(
        lambda *refs: difference_kernel(rim, psf_rim, *refs),
        out_shape=(
            jax.ShapeDtypeStruct((image_rows, image_cols), jnp.float32),
            jax.ShapeDtypeStruct(((rounded_rows + 2) * blocks, LANES), jnp.float32),
            jax.ShapeDtypeStruct((8, LANES), jnp.float32),
        ),
        in_specs=[vmem] * 5,
        out_specs=(vmem, vmem, vmem),
        scratch_shapes=[
            pltpu.VMEM(((image_rows + 2 * edge + 2) * blocks, LANES), jnp.float32),
            pltpu.VMEM((2, 2, 2, (image_rows + 2 * edge) // 8 * 16, 256), jnp.bfloat16),
            pltpu.VMEM((rounded_rows * blocks, LANES), jnp.float32),
        ],
        compiler_params=pltpu.CompilerParams(vmem_limit_bytes=20 * 2**20),
        cost_estimate=cost(14),
        name="difference",
    )(canvas, inner_rows, outer_rows, science, model_bands)

    totals = [square]
    for turn in (3, 1, 2):
        links = [(g[i], g[(i + turn) % PIECES]) for g in groups for i in range(PIECES)]
        totals.append(lax.ppermute(square, "visit", links))

    response = pl.pallas_call(
        response_kernel,
        out_shape=jax.ShapeDtypeStruct((image_rows, image_cols), jnp.float32),
        in_specs=[vmem, vmem],
        out_specs=vmem,
        scratch_shapes=[
            pltpu.VMEM((2, 2, 2, rounded_rows // 8 * 16, 256), jnp.bfloat16),
            pltpu.VMEM((image_rows * blocks, LANES), jnp.float32),
        ],
        compiler_params=pltpu.CompilerParams(vmem_limit_bytes=16 * 2**20),
        cost_estimate=cost(5),
        name="response",
    )(rounded, psf_bands)
    count = float(PIECES * image_rows * image_cols)
    detection = pl.pallas_call(
        lambda *refs: detection_kernel(count, *refs),
        out_shape=jax.ShapeDtypeStruct((image_rows, image_cols), jnp.float32),
        in_specs=[vmem] * (1 + PIECES),
        out_specs=vmem,
        compiler_params=pltpu.CompilerParams(vmem_limit_bytes=8 * 2**20),
        cost_estimate=cost(4),
        name="detection",
    )(response, *totals)
    return (difference, detection)


def solution(mesh):
    return jax.shard_map(
        shards,
        mesh=mesh,
        in_specs=(
            P(("groups", "visit"), None),
            P(("groups", "visit"), None),
            P("groups"),
            P(("groups", "visit"), None),
            P(("groups", "visit"), None),
            P(("groups", "visit"), None),
            P(),
            P(),
            P("groups", None),
            P(),
        ),
        out_specs=(P(("groups", "visit"), None), P(("groups", "visit"), None)),
        check_vma=False,
    )
```

profile of v0, /device:TPU:0, one launch (start us, length us, event | category | flops | bytes accessed | tf_op | source)
XLA Modules:
  0.0 55.2 jit_solution(11297900919601821719)
XLA Ops:
  0.6 0.0 copy-start
  0.6 0.0 copy-start.2
  0.7 0.0 copy-start.8
  0.7 0.0 copy-start.9
  0.7 0.0 copy-start.7
  0.7 0.0 copy-start.1
  0.7 3.1 %collective-permute-start.1 = (bf16[256,1024]{1,0:T(8,128)(2,1)}, bf16[256,1024]{1,0:T(8,128)(2,1)S(1)}, u32[]{:S(2)}, u32[]{:S(2)}) collective-permute-start(bf16[256,1024]{1,0:T(8,128)(2,1)} %own_piece.1), channel_id=1, source_target_pairs={{0,2},{1,3},{2,0},{3,1},{4,6},{5,7},{6,4},{7,5},{8,10},{9,11},{10,... | collective-permute-start | bytes 1572872 | tf_op jit(solution)/shard_map/ppermute | solution.py:42
  3.8 0.7 %collective-permute-start.3 = (bf16[256,1024]{1,0:T(8,128)(2,1)}, bf16[256,1024]{1,0:T(8,128)(2,1)S(1)}, u32[]{:S(2)}, u32[]{:S(2)}) collective-permute-start(bf16[256,1024]{1,0:T(8,128)(2,1)} %own_piece.1), channel_id=1, source_target_pairs={{1,4},{3,6},{4,1},{5,8},{6,3},{7,10},{8,5},{9,12},{10,7},{11,14},{... | collective-permute-start | bytes 1572872 | tf_op jit(solution)/shard_map/ppermute | solution.py:42
  4.4 11.4 %collective-permute-done.1.refs_1_.pair = bf16[256,1024]{1,0:T(8,128)(2,1)S(1)} collective-permute-done((bf16[256,1024]{1,0:T(8,128)(2,1)}, bf16[256,1024]{1,0:T(8,128)(2,1)S(1)}, u32[]{:S(2)}, u32[]{:S(2)}) %collective-permute-start.1) | collective-permute-done | bytes 524320 | tf_op jit(solution)/shard_map/ppermute | solution.py:42
  15.9 0.0 collective-permute-done.3.refs_3_.far
  15.9 0.0 copy-start.3
  15.9 0.0 copy-start.4
  16.0 0.0 copy-start.5
  16.0 0.0 copy-start.6
  16.0 4.7 %collective-permute-start.4 = (bf16[256,1024]{1,0:T(8,128)(2,1)S(1)}, bf16[256,1024]{1,0:T(8,128)(2,1)}, u32[]{:S(2)}, u32[]{:S(2)}) collective-permute-start(bf16[256,1024]{1,0:T(8,128)(2,1)S(1)} %relay.1), channel_id=1, source_target_pairs={{0,4},{1,2},{2,1},{4,8},{5,6},{6,5},{7,3},{8,12},{9,10},{10,9},{11... | collective-permute-start | bytes 1572872 | tf_op jit(solution)/shard_map/ppermute | solution.py:42
  20.6 0.0 copy-done.2
  20.6 0.0 collective-permute-start
  20.6 0.0 copy-done
  20.7 0.0 copy-done.8
  20.7 0.0 copy-done.9
  20.7 0.2 fusion
  20.9 0.5 collective-permute-start.2
  21.4 5.1 %collective-permute-done.4.piece = bf16[256,1024]{1,0:T(8,128)(2,1)} collective-permute-done((bf16[256,1024]{1,0:T(8,128)(2,1)S(1)}, bf16[256,1024]{1,0:T(8,128)(2,1)}, u32[]{:S(2)}, u32[]{:S(2)}) %collective-permute-start.4) | collective-permute-done | bytes 524320 | tf_op jit(solution)/shard_map/ppermute | solution.py:42
  26.5 0.3 collective-permute-start.5
  26.8 0.0 copy-done.7
  26.9 0.1 pad.1.clone
  26.9 0.1 pad.4.clone
  27.0 0.1 slice.35
  27.1 0.1 slice.29
  27.2 0.1 slice.31
  27.2 0.1 slice.33
  27.3 0.1 slice.25
  27.4 0.1 slice.27
  27.4 0.1 pad_maximum_fusion.1.psf_taps
  27.5 0.1 pad_maximum_fusion.model_taps
  27.6 0.0 copy-done.1
  27.6 1.2 %prepare.1 = (bf16[2,12,256,256]{3,2,1,0:T(8,128)(2,1)S(1)}, bf16[2,6,256,256]{3,2,1,0:T(8,128)(2,1)S(1)}, bf16[8,8,128]{2,1,0:T(8,128)(2,1)S(1)}, bf16[8,8,128]{2,1,0:T(8,128)(2,1)S(1)}) custom-call(f32[21,128]{1,0:T(8,128)S(1)} %pad_maximum_fusion.model_taps, f32[9,128]{1,0:T(8,128)S(1)} %pad_maximum_fusion.1.psf_taps, f32[256,1024]{1,0:T(8,128)S(1)} %copy-done.1, ...), custom_call_target="tpu_custom_call" | custom-call | bytes 4194304 | tf_op jit(solution)/shard_map/prepare/pallas_call | solution.py:448
  28.8 0.0 collective-permute-done.refs_0_
  28.8 0.0 collective-permute-done.2.refs_2_
  28.8 0.0 copy-done.3
  28.8 0.0 copy-done.4
  28.8 0.0 copy-done.5
  28.8 0.0 copy-done.6
  28.8 5.3 %near.1 = (f32[256,8,128]{2,1,0:T(8,128)S(1)}, f32[256,8,128]{2,1,0:T(8,128)S(1)}) custom-call(s32[1,4]{1,0:T(1,128)S(1)} %copy-done.3, s32[16]{0:T(128)S(1)} %copy-done.4, s32[1,4]{1,0:T(1,128)S(1)} %copy-done.5, s32[1,4]{1,0:T(1,128)S(1)} %copy-done.6, bf16[256,1024]{1,0:T(8,128)(2,1)S(1)} %copy-done.2, bf16[256,1024]{1,0:T(8,128)(2,1)} %collective-permute-done.refs_0_, ...), custom_call_target="tpu_custom_call" | custom-call | bytes 11534336 | tf_op jit(solution)/shard_map/near/pallas_call | solution.py:473
  34.1 1.4 %relayed.1.partial = f32[256,8,128]{2,1,0:T(8,128)S(1)} custom-call(s32[1,4]{1,0:T(1,128)S(1)} %copy-done.3, s32[16]{0:T(128)S(1)} %copy-done.4, s32[1,4]{1,0:T(1,128)S(1)} %copy-done.5, s32[1,4]{1,0:T(1,128)S(1)} %copy-done.6, f32[256,8,128]{2,1,0:T(8,128)S(1)} %get-tuple-element.14.partial, bf16[256,1024]{1,0:T(8,128)(2,1)} %collective-permute-done.4.piece), custom_call_target="tpu_custom_call" | custom-call | bytes 5242880 | tf_op jit(solution)/shard_map/relayed/pallas_call | solution.py:486
  35.5 0.0 collective-permute-done.5.piece
  35.5 1.0 %canvas.1 = (f32[256,8,128]{2,1,0:T(8,128)S(1)}, bf16[22,8,128]{2,1,0:T(8,128)(2,1)S(1)}, bf16[22,8,128]{2,1,0:T(8,128)(2,1)S(1)}) custom-call(s32[1,4]{1,0:T(1,128)S(1)} %copy-done.3, s32[16]{0:T(128)S(1)} %copy-done.4, s32[1,4]{1,0:T(1,128)S(1)} %copy-done.5, s32[1,4]{1,0:T(1,128)S(1)} %copy-done.6, f32[256,8,128]{2,1,0:T(8,128)S(1)} %relayed.1.partial, ...), custom_call_target="tpu_custom_call" | custom-call | bytes 5242880 | tf_op jit(solution)/shard_map/canvas/pallas_call | solution.py:496
  36.5 1.9 %collective-permute-start.6 = (bf16[22,8,128]{2,1,0:T(8,128)(2,1)S(1)}, bf16[22,8,128]{2,1,0:T(8,128)(2,1)S(1)}, u32[]{:S(2)}, u32[]{:S(2)}) collective-permute-start(bf16[22,8,128]{2,1,0:T(8,128)(2,1)S(1)} %get-tuple-element.19), channel_id=1, source_target_pairs={{0,1},{1,0},{4,5},{5,4},{8,9},{9,8},{12,13},{13,12},{16,17},{17,16... | collective-permute-start | bytes 135176 | tf_op jit(solution)/shard_map/ppermute | solution.py:510
  38.4 3.4 %collective-permute-start.7 = (bf16[22,8,128]{2,1,0:T(8,128)(2,1)S(1)}, bf16[22,8,128]{2,1,0:T(8,128)(2,1)S(1)}, u32[]{:S(2)}, u32[]{:S(2)}) collective-permute-start(bf16[22,8,128]{2,1,0:T(8,128)(2,1)S(1)} %get-tuple-element.20), channel_id=1, source_target_pairs={{15,0},{0,15},{1,2},{2,1},{3,4},{4,3},{5,6},{6,5},{7,8},{8,7},{9,1... | collective-permute-start | bytes 135176 | tf_op jit(solution)/shard_map/ppermute | solution.py:510
  41.9 0.0 collective-permute-done.6.refs_1_
  41.9 2.8 %collective-permute-done.7.refs_2_ = bf16[22,8,128]{2,1,0:T(8,128)(2,1)S(1)} collective-permute-done((bf16[22,8,128]{2,1,0:T(8,128)(2,1)S(1)}, bf16[22,8,128]{2,1,0:T(8,128)(2,1)S(1)}, u32[]{:S(2)}, u32[]{:S(2)}) %collective-permute-start.7) | collective-permute-done | bytes 45088 | tf_op jit(solution)/shard_map/ppermute | solution.py:510
  44.7 3.7 %difference.1 = (f32[256,1024]{1,0:T(8,128)}, f32[2128,128]{1,0:T(8,128)S(1)}, f32[8,128]{1,0:T(8,128)S(1)}) custom-call(f32[256,8,128]{2,1,0:T(8,128)S(1)} %get-tuple-element.18.refs_0_, bf16[22,8,128]{2,1,0:T(8,128)(2,1)S(1)} %collective-permute-done.6.refs_1_, bf16[22,8,128]{2,1,0:T(8,128)(2,1)S(1)} %collective-permute-done.7.refs_2_, ...), custom_call_target="tpu_custom_call" | custom-call | bytes 14680064 | tf_op jit(solution)/shard_map/difference/pallas_call | solution.py:516
  48.4 0.0 collective-permute-start.10
  48.4 3.5 %collective-permute-start.9 = (f32[8,128]{1,0:T(8,128)S(1)}, f32[8,128]{1,0:T(8,128)S(1)}, u32[]{:S(2)}, u32[]{:S(2)}) collective-permute-start(f32[8,128]{1,0:T(8,128)S(1)} %get-tuple-element.25.refs_1_), channel_id=1, source_target_pairs={{15,0},{0,1},{1,2},{2,15},{3,4},{4,5},{5,6},{6,3},{7,8},{8,9},{9,1... | collective-permute-start | bytes 12296 | tf_op jit(solution)/shard_map/ppermute | solution.py:538
  51.9 1.0 %collective-permute-start.8 = (f32[8,128]{1,0:T(8,128)S(1)}, f32[8,128]{1,0:T(8,128)S(1)}, u32[]{:S(2)}, u32[]{:S(2)}) collective-permute-start(f32[8,128]{1,0:T(8,128)S(1)} %get-tuple-element.25.refs_1_), channel_id=1, source_target_pairs={{15,2},{0,15},{1,0},{2,1},{3,6},{4,3},{5,4},{6,5},{7,10},{8,7},{9,... | collective-permute-start | bytes 12296 | tf_op jit(solution)/shard_map/ppermute | solution.py:538
  52.8 1.3 %response.1.refs_0_ = f32[256,1024]{1,0:T(8,128)S(1)} custom-call(f32[2128,128]{1,0:T(8,128)S(1)} %get-tuple-element.23.rounded, bf16[2,6,256,256]{3,2,1,0:T(8,128)(2,1)S(1)} %get-tuple-element.24.bands), custom_call_target="tpu_custom_call" | custom-call | bytes 5242880 | tf_op jit(solution)/shard_map/response/pallas_call | solution.py:540
  54.1 0.0 collective-permute-done.10.refs_4_
  54.1 0.0 collective-permute-done.9.refs_3_
  54.1 0.0 collective-permute-done.8.refs_2_
  54.1 1.1 %detection.1 = f32[256,1024]{1,0:T(8,128)} custom-call(f32[256,1024]{1,0:T(8,128)S(1)} %response.1.refs_0_, f32[8,128]{1,0:T(8,128)S(1)} %get-tuple-element.25.refs_1_, f32[8,128]{1,0:T(8,128)S(1)} %collective-permute-done.8.refs_2_, f32[8,128]{1,0:T(8,128)S(1)} %collective-permute-done.9.refs_3_, f32[8,128]{1,0:T(8,128)S(1)} %collective-permute-done.10.refs_4_), custom_call_target="tpu_custom_call" | custom-call | bytes 4194304 | tf_op jit(solution)/shard_map/detection/pallas_call | solution.py:554
  (5 shorter events, 0.0 us)
Async XLA Ops:
  0.6 20.0 %copy-start = (f32[4,20]{1,0:T(4,128)S(1)}, f32[4,20]{1,0:T(4,128)}, u32[]{:S(2)}) copy-start(f32[4,20]{1,0:T(4,128)} %param.18) | copy-start | bytes 964
  0.6 20.0 %copy-start.2 = (bf16[256,1024]{1,0:T(8,128)(2,1)S(1)}, bf16[256,1024]{1,0:T(8,128)(2,1)}, u32[]{:S(2)}) copy-start(bf16[256,1024]{1,0:T(8,128)(2,1)} %own_piece.1) | copy-start | bytes 1572868
  0.7 20.0 %copy-start.8 = (f32[20,21]{1,0:T(8,128)S(1)}, f32[20,21]{1,0:T(8,128)}, u32[]{:S(2)}) copy-start(f32[20,21]{1,0:T(8,128)} %param.17) | copy-start | bytes 5044
  0.7 20.0 %copy-start.9 = (f32[20,21]{1,0:T(8,128)S(1)}, f32[20,21]{1,0:T(8,128)}, u32[]{:S(2)}) copy-start(f32[20,21]{1,0:T(8,128)} %param.16) | copy-start | bytes 5044
  0.7 26.2 %copy-start.7 = (f32[9,9]{1,0:T(8,128)S(1)}, f32[9,9]{1,0:T(8,128)}, u32[]{:S(2)}) copy-start(f32[9,9]{1,0:T(8,128)} %param.19) | copy-start | bytes 976
  0.7 26.9 %copy-start.1 = (f32[256,1024]{1,0:T(8,128)S(1)}, f32[256,1024]{1,0:T(8,128)}, u32[]{:S(2)}) copy-start(f32[256,1024]{1,0:T(8,128)} %refs_3_.1) | copy-start | bytes 3145732
  0.7 15.2 %collective-permute-start.1 = (bf16[256,1024]{1,0:T(8,128)(2,1)}, bf16[256,1024]{1,0:T(8,128)(2,1)S(1)}, u32[]{:S(2)}, u32[]{:S(2)}) collective-permute-start(bf16[256,1024]{1,0:T(8,128)(2,1)} %own_piece.1), channel_id=1, source_target_pairs={{0,2},{1,3},{2,0},{3,1},{4,6},{5,7},{6,4},{7,5},{8,10},{9,11},{10,... | collective-permute-start | bytes 1572872 | tf_op jit(solution)/shard_map/ppermute | solution.py:42
  3.8 12.1 %collective-permute-start.3 = (bf16[256,1024]{1,0:T(8,128)(2,1)}, bf16[256,1024]{1,0:T(8,128)(2,1)S(1)}, u32[]{:S(2)}, u32[]{:S(2)}) collective-permute-start(bf16[256,1024]{1,0:T(8,128)(2,1)} %own_piece.1), channel_id=1, source_target_pairs={{1,4},{3,6},{4,1},{5,8},{6,3},{7,10},{8,5},{9,12},{10,7},{11,14},{... | collective-permute-start | bytes 1572872 | tf_op jit(solution)/shard_map/ppermute | solution.py:42
  15.9 12.9 %copy-start.3 = (s32[1,4]{1,0:T(1,128)S(1)}, s32[1,4]{1,0:T(1,128)}, u32[]{:S(2)}) copy-start(s32[1,4]{1,0:T(1,128)} %covering.5) | copy-start | bytes 52
  15.9 12.9 %copy-start.4 = (s32[16]{0:T(128)S(1)}, s32[16]{0:T(128)}, u32[]{:S(2)}) copy-start(s32[16]{0:T(128)} %owner_map.5) | copy-start | bytes 196
  16.0 12.9 %copy-start.5 = (s32[1,4]{1,0:T(1,128)S(1)}, s32[1,4]{1,0:T(1,128)}, u32[]{:S(2)}) copy-start(s32[1,4]{1,0:T(1,128)} %row_shift.5) | copy-start | bytes 52
  16.0 12.9 %copy-start.6 = (s32[1,4]{1,0:T(1,128)S(1)}, s32[1,4]{1,0:T(1,128)}, u32[]{:S(2)}) copy-start(s32[1,4]{1,0:T(1,128)} %col_shift.5) | copy-start | bytes 52
  16.0 10.5 %collective-permute-start.4 = (bf16[256,1024]{1,0:T(8,128)(2,1)S(1)}, bf16[256,1024]{1,0:T(8,128)(2,1)}, u32[]{:S(2)}, u32[]{:S(2)}) collective-permute-start(bf16[256,1024]{1,0:T(8,128)(2,1)S(1)} %relay.1), channel_id=1, source_target_pairs={{0,4},{1,2},{2,1},{4,8},{5,6},{6,5},{7,3},{8,12},{9,10},{10,9},{11... | collective-permute-start | bytes 1572872 | tf_op jit(solution)/shard_map/ppermute | solution.py:42
  20.6 8.1 %collective-permute-start = (bf16[256,1024]{1,0:T(8,128)(2,1)S(1)}, bf16[256,1024]{1,0:T(8,128)(2,1)}, u32[]{:S(2)}, u32[]{:S(2)}) collective-permute-start(bf16[256,1024]{1,0:T(8,128)(2,1)S(1)} %copy-done.2), channel_id=1, source_target_pairs={{0,1},{1,0},{2,3},{3,2},{4,5},{5,4},{6,7},{7,6},{8,9},{9,8},{10,11... | collective-permute-start | bytes 1572872 | tf_op jit(solution)/shard_map/ppermute | solution.py:42
  20.9 7.9 %collective-permute-start.2 = (bf16[256,1024]{1,0:T(8,128)(2,1)S(1)}, bf16[256,1024]{1,0:T(8,128)(2,1)}, u32[]{:S(2)}, u32[]{:S(2)}) collective-permute-start(bf16[256,1024]{1,0:T(8,128)(2,1)S(1)} %collective-permute-done.1.refs_1_.pair), channel_id=1, source_target_pairs={{0,1},{1,0},{2,3},{3,2},{4,5},{5,4},{6,7},{7,6},{8,9},{9,8},{10,11... | collective-permute-start | bytes 1572872 | tf_op jit(solution)/shard_map/ppermute | solution.py:42
  26.5 9.0 %collective-permute-start.5 = (bf16[256,1024]{1,0:T(8,128)(2,1)}, bf16[256,1024]{1,0:T(8,128)(2,1)S(1)}, u32[]{:S(2)}, u32[]{:S(2)}) collective-permute-start(bf16[256,1024]{1,0:T(8,128)(2,1)} %collective-permute-done.4.piece), channel_id=1, source_target_pairs={{0,1},{1,0},{2,3},{3,2},{4,5},{5,4},{6,7},{7,6},{8,9},{9,8},{10,11... | collective-permute-start | bytes 1572872 | tf_op jit(solution)/shard_map/ppermute | solution.py:42
  36.5 5.4 %collective-permute-start.6 = (bf16[22,8,128]{2,1,0:T(8,128)(2,1)S(1)}, bf16[22,8,128]{2,1,0:T(8,128)(2,1)S(1)}, u32[]{:S(2)}, u32[]{:S(2)}) collective-permute-start(bf16[22,8,128]{2,1,0:T(8,128)(2,1)S(1)} %get-tuple-element.19), channel_id=1, source_target_pairs={{0,1},{1,0},{4,5},{5,4},{8,9},{9,8},{12,13},{13,12},{16,17},{17,16... | collective-permute-start | bytes 135176 | tf_op jit(solution)/shard_map/ppermute | solution.py:510
  38.4 6.2 %collective-permute-start.7 = (bf16[22,8,128]{2,1,0:T(8,128)(2,1)S(1)}, bf16[22,8,128]{2,1,0:T(8,128)(2,1)S(1)}, u32[]{:S(2)}, u32[]{:S(2)}) collective-permute-start(bf16[22,8,128]{2,1,0:T(8,128)(2,1)S(1)} %get-tuple-element.20), channel_id=1, source_target_pairs={{15,0},{0,15},{1,2},{2,1},{3,4},{4,3},{5,6},{6,5},{7,8},{8,7},{9,1... | collective-permute-start | bytes 135176 | tf_op jit(solution)/shard_map/ppermute | solution.py:510
  48.4 5.7 %collective-permute-start.10 = (f32[8,128]{1,0:T(8,128)S(1)}, f32[8,128]{1,0:T(8,128)S(1)}, u32[]{:S(2)}, u32[]{:S(2)}) collective-permute-start(f32[8,128]{1,0:T(8,128)S(1)} %get-tuple-element.25.refs_1_), channel_id=1, source_target_pairs={{15,1},{0,2},{1,15},{2,0},{3,5},{4,6},{5,3},{6,4},{7,9},{8,10},{9,... | collective-permute-start | bytes 12296 | tf_op jit(solution)/shard_map/ppermute | solution.py:538
  48.4 5.8 %collective-permute-start.9 = (f32[8,128]{1,0:T(8,128)S(1)}, f32[8,128]{1,0:T(8,128)S(1)}, u32[]{:S(2)}, u32[]{:S(2)}) collective-permute-start(f32[8,128]{1,0:T(8,128)S(1)} %get-tuple-element.25.refs_1_), channel_id=1, source_target_pairs={{15,0},{0,1},{1,2},{2,15},{3,4},{4,5},{5,6},{6,3},{7,8},{8,9},{9,1... | collective-permute-start | bytes 12296 | tf_op jit(solution)/shard_map/ppermute | solution.py:538
  51.9 2.3 %collective-permute-start.8 = (f32[8,128]{1,0:T(8,128)S(1)}, f32[8,128]{1,0:T(8,128)S(1)}, u32[]{:S(2)}, u32[]{:S(2)}) collective-permute-start(f32[8,128]{1,0:T(8,128)S(1)} %get-tuple-element.25.refs_1_), channel_id=1, source_target_pairs={{15,2},{0,15},{1,0},{2,1},{3,6},{4,3},{5,4},{6,5},{7,10},{8,7},{9,... | collective-permute-start | bytes 12296 | tf_op jit(solution)/shard_map/ppermute | solution.py:538
where the time goes:
time: 55.7 us; the launch traced here: 55.2 us
  waiting for transfers between devices  19.3 us (35%)
  starting transfers between devices  19 us (34%)
  Pallas kernels  14.9 us (27%)
  between operations  0.88 us (2%)
  local copies, waits for them, and re-layouts  0.65 us (1%)
    ppermute x6, waiting for transfers between devices, move(): return lax.ppermute(value, 'visit', kept)  16.5 us
    ppermute x6, starting transfers between devices, move(): return lax.ppermute(value, 'visit', kept)  9.23 us
    ppermute x2, starting transfers between devices, swap(): lax.ppermute(value, 'visit', [(g[a], g[b]) for g in groups for a, b in pa...  5.37 us
    pallas_call x1, Pallas kernels, shards(): pl.pallas_call(near_kernel, out_shape=(canvas_shape, canvas_shape), in_sp...  5.29 us
    ppermute x3, starting transfers between devices, shards(): totals.append(lax.ppermute(square, 'visit', links))  4.45 us
    pallas_call x1, Pallas kernels, shards(): pl.pallas_call(lambda *refs: difference_kernel(rim, psf_rim, *refs), out_...  3.7 us
    ppermute x2, waiting for transfers between devices, swap(): lax.ppermute(value, 'visit', [(g[a], g[b]) for g in groups for a, b in pa...  2.79 us
    pallas_call x1, Pallas kernels, shards(): pl.pallas_call(relayed_kernel, out_shape=canvas_shape, in_specs=[smem] *...  1.37 us
  transfers between devices with their start and end apart: 11, of which 3 were waited for; matrix products, arithmetic and copies ran while one was open for 2% of the time, Pallas kernels for 17%

commit v1 on v0

v1 whole, which is shorter than its diff:
```python
import jax
import jax.numpy as jnp
from jax import lax
from jax.experimental import pallas as pl
from jax.experimental.pallas import tpu as pltpu
from jax.sharding import PartitionSpec as P


PIECES = 4
SUMS = (((0, 2), (1, 3)), ((0, 1), (2, 3)), ((0, 3), (1, 2)))
LANES = 128

BUFFER_OF = ((4, 5, 6, 0, 1, 2, 3), (6, 5, 1, 0, 3, 2, 4), (4, 2, 3, 0, 1, 5, 6), (3, 2, 1, 0, 6, 5, 4))


def cost(megabytes):
    return pl.CostEstimate(flops=0, transcendentals=0, bytes_accessed=megabytes * 2**20)


def relay_kernel(far, pair, out):
    residue = lax.rem(lax.axis_index("visit"), 4)
    passes_far = (residue == 1) | (residue == 2)

    @pl.when(passes_far)
    def _():
        out[...] = far[...]

    @pl.when(jnp.logical_not(passes_far))
    def _():
        out[...] = pair[...]


def place_of():
    devices = lax.axis_size("visit")
    return lax.rem(lax.rem(lax.axis_index("visit") + 1, devices), PIECES)


def gather_pieces(own):
    count = lax.axis_size("visit")

    def move(value, pairs):
        kept = [(i, j) for i, j in pairs if 0 <= j < count]
        return lax.ppermute(value, "visit", kept)

    pair = move(own, [(i, i ^ 2) for i in range(count)])
    far = move(own, [(i, i + 3 if i % 2 else i - 3) for i in range(count)])
    partner = move(own, [(i, i ^ 1) for i in range(count)])
    whole = pl.BlockSpec(memory_space=pltpu.VMEM)
    relay = pl.pallas_call(
        relay_kernel,
        out_shape=jax.ShapeDtypeStruct(own.shape, own.dtype),
        in_specs=[whole, whole],
        out_specs=whole,
        compiler_params=pltpu.CompilerParams(vmem_limit_bytes=4 * 2**20),
        cost_estimate=cost(1),
        name="relay",
    )(far, pair)
    targets = {0: 4, 1: 1, 2: -1, 3: -4}
    relayed = move(relay, [(i, i + targets[i % 4]) for i in range(count)])
    crossed = move(pair, [(i, i ^ 1) for i in range(count)])
    relayed_crossed = move(relayed, [(i, i ^ 1) for i in range(count)])
    return (own, partner, pair, crossed, far, relayed, relayed_crossed)


CHUNK = 16
EDGE = 16


def spread(piece, turn, target, first):
    rows, cols = piece.shape
    blocks = cols // LANES

    def body(step, carry):
        row = pl.multiple_of(step * CHUNK, CHUNK)
        for k in range(blocks):
            tile = piece[pl.ds(row, CHUNK), k * LANES : (k + 1) * LANES].astype(jnp.float32)
            if turn is not None:
                tile = pltpu.roll(tile, turn, 1)
            target[pl.ds(first + row * blocks + k, CHUNK, stride=blocks), :] = tile
        return carry

    lax.fori_loop(0, rows // CHUNK, body, 0, unroll=4)


def shift_of(rows, blocks, row_shift, col_shift, valid):
    most = rows // 2
    base = (most + 1) * blocks
    lane = lax.broadcasted_iota(jnp.int32, (blocks, LANES), 1)
    block = lax.broadcasted_iota(jnp.int32, (blocks, LANES), 0)
    back = -col_shift
    start = lax.shift_right_arithmetic(back, 7)
    left = back - start * LANES
    turn = lax.bitwise_and(LANES - left, LANES - 1)
    limit = jnp.where(valid, blocks, -2 * blocks)
    here = block + start
    masks = (
        (lane < LANES - left) & (here >= 0) & (here < limit),
        (lane >= LANES - left) & (here >= -1) & (here < limit - 1),
    )
    return base, turn, base - row_shift * blocks + start, masks


def clear_ends(moved, rows, blocks):
    pad = rows // 2 * blocks
    base = pad + blocks
    moved[blocks:base, :] = jnp.zeros((pad, LANES), jnp.float32)
    moved[base + rows * blocks : base + rows * blocks + pad, :] = jnp.zeros((pad, LANES), jnp.float32)


def add_moved(rows, blocks, read, moves, write):
    def body(step, carry):
        for i in range(8):
            row = step * 8 + i
            value = read(row)
            for moved, start, masks in moves:
                low = moved[pl.ds(start + row * blocks, blocks), :]
                high = moved[pl.ds(start + row * blocks + 1, blocks), :]
                value = value + jnp.where(masks[0], low, jnp.where(masks[1], high, 0.0))
            write(row, value)
        return carry

    lax.fori_loop(0, rows // 8, body, 0, unroll=4)


def slot_of(covering, owner_map, slot):
    position = lax.axis_index("visit")
    residue = lax.rem(position, 4)
    distance = owner_map[covering[0, slot]] - position
    buffer = jnp.int32(0)
    for place, row in enumerate(BUFFER_OF):
        for index, held in enumerate(row):
            here = (residue == place) & (distance == index - len(row) // 2)
            buffer = jnp.where(here, held, buffer)
    return buffer


def near_kernel(table, own, *refs):
    pieces, (out, recip, moved) = refs[:4], refs[4:]
    rows, cols = pieces[0].shape
    blocks = cols // LANES
    slots = moved.shape[0]
    moves = []
    for slot in range(slots):
        held = table[0, slot]
        base, turn, start, masks = shift_of(
            rows, blocks, table[0, slots + slot], table[0, 2 * slots + slot], held <= len(pieces)
        )
        clear_ends(moved.at[slot], rows, blocks)
        for index in range(len(pieces)):

            @pl.when(held == index + 1)
            def _():
                spread(pieces[index], turn, moved.at[slot], base)

        moves.append((moved.at[slot], start, masks))

    def read(row):
        return own[pl.ds(pl.multiple_of(row * blocks, blocks), blocks), :]

    def write(row, value):
        out[row] = value

    add_moved(rows, blocks, read, moves, write)
    column = lax.broadcasted_iota(jnp.int32, (blocks, LANES), 0) * LANES
    column = column + lax.broadcasted_iota(jnp.int32, (blocks, LANES), 1)
    covers = []
    for slot in range(slots):
        source = column - table[0, 2 * slots + slot]
        covers.append(jnp.where((source >= 0) & (source < cols), 1.0, 0.0))

    def cover(step, carry):
        for i in range(8):
            row = step * 8 + i
            total = jnp.ones((blocks, LANES), jnp.float32)
            for slot in range(slots):
                source = row - table[0, slots + slot]
                inside = ((source >= 0) & (source < rows)).astype(jnp.float32)
                total = total + covers[slot] * inside
            recip[row] = 1.0 / total
        return carry

    lax.fori_loop(0, rows // 8, cover, 0, unroll=4)


def relayed_kernel(table, partial, piece, out, moved):
    rows, blocks, _ = partial.shape
    first = table.shape[1] - 6
    valid = table[0, first] > 0
    base, turn, start, masks = shift_of(rows, blocks, table[0, first + 1], table[0, first + 2], valid)

    @pl.when(valid)
    def _():
        clear_ends(moved, rows, blocks)
        spread(piece, turn, moved, base)

    def write(row, value):
        out[row] = value

    add_moved(rows, blocks, lambda row: partial[row], [(moved, start, masks)], write)


def canvas_kernel(
    table, partial, piece, recip, first_rows, last_rows, out, to_inner, to_outer, moved,
):
    rows, blocks, _ = partial.shape
    first = table.shape[1] - 3
    valid = table[0, first] > 0
    base, turn, start, masks = shift_of(rows, blocks, table[0, first + 1], table[0, first + 2], valid)

    @pl.when(valid)
    def _():
        clear_ends(moved, rows, blocks)
        spread(piece, turn, moved, base)

    def write(row, value):
        out[pl.ds(pl.multiple_of(row * blocks, blocks), blocks), :] = value * recip[row]

    add_moved(rows, blocks, lambda row: partial[row], [(moved, start, masks)], write)

    def rows_of(first, count):
        return out[first * blocks : (first + count) * blocks, :].reshape(count, blocks, LANES).astype(jnp.bfloat16)

    edge = to_inner.shape[0] - first_rows.shape[0]
    even = lax.rem(place_of(), 2) == 0
    for message, up in ((to_inner, even), (to_outer, jnp.logical_not(even))):

        @pl.when(up)
        def _():
            message[:edge] = rows_of(0, edge)
            message[edge:] = first_rows[...]

        @pl.when(jnp.logical_not(up))
        def _():
            message[:edge] = rows_of(rows - edge, edge)
            message[edge:] = last_rows[...]


def bands_of(taps, bands):
    count, lanes = taps.shape
    half = lanes // 2
    lower = lax.broadcasted_iota(jnp.int32, (lanes, lanes), 1) < half
    zero = jnp.zeros((lanes, lanes), jnp.float32)

    def table(tap, shift):
        if not 0 <= tap < count:
            return zero
        spread = jnp.broadcast_to(taps[tap : tap + 1, :], (lanes, lanes))
        return pltpu.roll(spread, shift, 1, stride=1, stride_axis=0)

    for offset in range(2 * bands.shape[1]):
        at = slice((offset % 2) * lanes, (offset % 2 + 1) * lanes)
        for pair in range(2):
            plain = table(offset - 2 * pair, 0)
            turned = table(offset - 2 * pair - 1, half)
            to = slice(pair * lanes, (pair + 1) * lanes)
            bands[0, offset // 2, at, to] = jnp.where(lower, plain, turned).astype(bands.dtype)
            bands[1, offset // 2, at, to] = jnp.where(lower, turned, plain).astype(bands.dtype)


def prepare_kernel(
    covering_in, owner_in, row_in, col_in, model_taps, psf_taps, science_in, piece_in,
    table, model_bands, psf_bands, first_rows, last_rows, turned, own,
    covering, owner_map, row_shift, col_shift, science, piece, arrived,
):
    sources = (covering_in, owner_in, row_in, col_in, science_in, piece_in)
    copies = [
        pltpu.make_async_copy(source, target, arrived.at[index])
        for index, (source, target) in enumerate(
            zip(sources, (covering, owner_map, row_shift, col_shift, science, piece))
        )
    ]
    for copy in copies:
        copy.start()
    bands_of(model_taps, model_bands)
    bands_of(psf_taps, psf_bands)
    for copy in copies:
        copy.wait()
    slots = covering.shape[1] - 1
    late = [[jnp.int32(0)] * 3 for _ in range(2)]
    for slot in range(slots):
        held = slot_of(covering, owner_map, slot + 1)
        entry = (held, row_shift[0, slot + 1], col_shift[0, slot + 1])
        for index in range(3):
            table[0, index * slots + slot] = entry[index]
        for buffer in range(2):
            here = held == 5 + buffer
            values = (jnp.int32(1), entry[1], entry[2])
            late[buffer] = [jnp.where(here, new, old) for new, old in zip(values, late[buffer])]
    for buffer in range(2):
        for index in range(3):
            table[0, 3 * (slots + buffer) + index] = late[buffer][index]
    spread(piece, None, own, 0)
    rows, cols = science.shape
    blocks = cols // LANES
    for row in range(0, rows, CHUNK):
        for k in range(blocks):
            at = pl.ds(row * blocks + k, CHUNK, stride=blocks)
            turned[at, :] = science[row : row + CHUNK, k * LANES : (k + 1) * LANES]
    count = first_rows.shape[0] // 2
    for out, first in ((first_rows, 0), (last_rows, rows - count)):
        for row in range(count):
            value = turned[(first + row) * blocks : (first + row + 1) * blocks, :]
            high = value.astype(jnp.bfloat16)
            out[row] = high
            out[count + row] = (value - high.astype(jnp.float32)).astype(jnp.bfloat16)


def pack_rows(source, start, steps, packed, base):
    blocks = 8
    lane = lax.broadcasted_iota(jnp.int32, (blocks, LANES), 1)
    block = lax.broadcasted_iota(jnp.int32, (blocks, LANES), 0)
    inner = block > 0
    outer = block < blocks - 1

    def sides(x):
        at = start + blocks * x
        here = source[at : at + blocks, :]
        before = source[at - 1 : at - 1 + blocks, :]
        after = source[at + 1 : at + 1 + blocks, :]
        return (
            jnp.where(lane < 96, here, jnp.where(inner, before, 0.0)),
            jnp.where(lane >= 32, here, jnp.where(outer, after, 0.0)),
        )

    for phase in range(4):
        last = sides(phase)
        for h in range(1, steps):
            now = sides(4 * h + phase)
            odd, p = (h - 1) % 2, base + (h - 1) // 2
            for side in range(2):
                tile = jnp.concatenate([last[side], now[side]], axis=0).astype(jnp.bfloat16)
                to = slice((phase % 2) * LANES, (phase % 2 + 1) * LANES)
                packed[odd, side, phase // 2, 16 * p : 16 * p + 16, to] = tile
            last = now


def product_of(packed, bands, side, parts):
    chunks = bands.shape[1]
    left = []
    for chunk in range(chunks):
        q, pair = chunk // 2, chunk % 2
        rows = []
        for base, groups in parts:
            first = 16 * (base + q // 2)
            rows.append(packed[q % 2, side, pair, first : first + 8 * groups, :])
        left.append(rows[0] if len(rows) == 1 else jnp.concatenate(rows, axis=0))
    right = bands[side].reshape(chunks * 256, 256)
    return jnp.dot(jnp.concatenate(left, axis=1), right, preferred_element_type=jnp.float32)


def unfold(packed, bands, parts, put):
    low = product_of(packed, bands, 0, parts)
    high = product_of(packed, bands, 1, parts)
    lower = lax.broadcasted_iota(jnp.int32, (8, LANES), 1) < LANES // 2
    for g in range(sum(groups for _, groups in parts)):
        rows = slice(8 * g, 8 * g + 8)
        for pair in range(2):
            lanes = slice(pair * LANES, (pair + 1) * LANES)
            a, b = low[rows, lanes], high[rows, lanes]
            put(4 * g + 2 * pair, jnp.where(lower, a, b))
            put(4 * g + 2 * pair + 1, pltpu.roll(jnp.where(lower, b, a), LANES // 2, 1))


def interior_kernel(
    rim, psf_rim, canvas, science, model_bands, psf_bands, difference, response, square, packed, packed_psf,
):
    blocks = 8
    rows = canvas.shape[0] // blocks
    first = EDGE - psf_rim
    groups = (rows - 2 * first) // 4
    pack_rows(canvas, (first - rim) * blocks, groups + model_bands.shape[1] // 2 - 1, packed, 0)
    totals = [jnp.zeros((blocks, LANES), jnp.float32) for _ in range(4)]

    def put(i, value):
        at = slice((first + i) * blocks, (first + i + 1) * blocks)
        value = science[at, :] - value
        difference[at, :] = value
        totals[i % 4] = totals[i % 4] + value * value

    unfold(packed, model_bands, [(0, groups)], put)
    square[...] = (totals[0] + totals[1]) + (totals[2] + totals[3])
    groups = (rows - 2 * EDGE) // 4
    pack_rows(difference, first * blocks, groups + psf_bands.shape[1] // 2 - 1, packed_psf, 0)

    def put_response(i, value):
        response[(EDGE + i) * blocks : (EDGE + i + 1) * blocks, :] = value

    unfold(packed_psf, psf_bands, [(0, groups)], put_response)


def edge_kernel(
    rim, psf_rim, canvas, inner_rows, outer_rows, science, bands, partial, top, bottom, square, joint, packed,
):
    blocks = 8
    rows = canvas.shape[0] // blocks
    edge = rim + psf_rim
    groups = EDGE // 4
    span = EDGE + 2 * rim
    starts = (blocks, (span + 3) * blocks)
    place = place_of()
    odd = lax.rem(place, 2) == 1
    own = span - edge
    joint[starts[0] + edge * blocks : starts[0] + span * blocks, :] = canvas[: own * blocks, :]
    joint[starts[1] : starts[1] + own * blocks, :] = canvas[(rows - own) * blocks :, :]
    for swapped in range(2):

        @pl.when(odd == (swapped == 1))
        def _():
            above, below = (outer_rows, inner_rows) if swapped else (inner_rows, outer_rows)
            to = starts[0]
            joint[to : to + edge * blocks, :] = above[:edge].astype(jnp.float32).reshape(-1, LANES)
            to = starts[1] + own * blocks
            joint[to : to + edge * blocks, :] = below[:edge].astype(jnp.float32).reshape(-1, LANES)
            for source, at in ((above, 0), (below, psf_rim)):
                value = source[edge : edge + psf_rim].astype(jnp.float32)
                value = value + source[edge + psf_rim : edge + 2 * psf_rim].astype(jnp.float32)
                to = (2 * (span + 3) + at) * blocks
                joint[to : to + psf_rim * blocks, :] = value.reshape(-1, LANES)

    steps = groups + bands.shape[1] // 2 - 1
    pairs = steps // 2
    pack_rows(joint, starts[0], steps, packed, 0)
    pack_rows(joint, starts[1], steps, packed, pairs)
    totals = [partial[...], jnp.zeros((blocks, LANES), jnp.float32)]

    def put(i, value):
        side, row = i // EDGE, i % EDGE
        target = (top, bottom)[side]
        at = slice(row * blocks, (row + 1) * blocks)
        outside = row < psf_rim if side == 0 else row >= EDGE - psf_rim
        if outside:
            which = row if side == 0 else psf_rim + row - (EDGE - psf_rim)
            to = (2 * (span + 3) + which) * blocks
            joined = place > 0 if side == 0 else place < PIECES - 1
            target[at, :] = jnp.where(joined, joint[to : to + blocks, :] - value, 0.0)
        else:
            to = (row - psf_rim if side == 0 else rows - EDGE + psf_rim + row) * blocks
            value = science[to : to + blocks, :] - value
            target[at, :] = value
            totals[side] = totals[side] + value * value

    unfold(packed, bands, [(0, groups), (pairs, groups)], put)
    square[...] = jnp.broadcast_to(jnp.sum(totals[0] + totals[1]), square.shape)


def rest_kernel(psf_rim, top, bottom, inside, bands, difference, response, joint, packed):
    blocks = 8
    rows, _ = difference.shape
    groups = EDGE // 4
    span = EDGE + 2 * psf_rim
    more = span - EDGE
    starts = (blocks, (span + 3) * blocks)
    joint[starts[0] : starts[0] + EDGE * blocks, :] = top[...]
    from_row = EDGE - psf_rim
    to = starts[0] + EDGE * blocks
    joint[to : to + more * blocks, :] = inside[from_row * blocks : (from_row + more) * blocks, :]
    from_row = rows - EDGE + psf_rim - more
    joint[starts[1] : starts[1] + more * blocks, :] = inside[from_row * blocks : (from_row + more) * blocks, :]
    joint[starts[1] + more * blocks : starts[1] + span * blocks, :] = bottom[...]
    steps = groups + bands.shape[1] // 2 - 1
    pairs = (steps + 1) // 2
    pack_rows(joint, starts[0], steps, packed, 0)
    pack_rows(joint, starts[1], steps, packed, pairs)

    def put(i, value):
        response[i * blocks : (i + 1) * blocks, :] = value

    unfold(packed, bands, [(0, groups), (pairs, groups)], put)
    for row in range(0, rows, 8):
        if row < EDGE:
            source, at = joint, starts[0] + (row + psf_rim) * blocks
        elif row >= rows - EDGE:
            source, at = joint, starts[1] + (row - (rows - EDGE - psf_rim)) * blocks
        else:
            source, at = inside, row * blocks
        for k in range(blocks):
            difference[row : row + 8, k * LANES : (k + 1) * LANES] = source[pl.ds(at + k, 8, stride=blocks), :]


def detection_kernel(count, inside, ends, *refs):
    out = refs[-1]
    total = refs[0][...]
    for ref in refs[1:-1]:
        total = total + ref[...]
    scale = 1.0 / jnp.sqrt(total / count + 1e-06)
    rows, cols = out.shape
    blocks = cols // LANES
    for row in range(0, rows, 8):
        if row < EDGE:
            source, at = ends, row * blocks
        elif row >= rows - EDGE:
            source, at = ends, (row - (rows - 2 * EDGE)) * blocks
        else:
            source, at = inside, row * blocks
        for k in range(blocks):
            out[row : row + 8, k * LANES : (k + 1) * LANES] = source[pl.ds(at + k, 8, stride=blocks), :] * scale


def tap_rows(taps, width):
    rim = taps.shape[1] // 2
    turned = jnp.flip(taps, axis=1)
    gap = jnp.zeros((taps.shape[0], width - taps.shape[1]), jnp.float32)
    return jnp.concatenate([turned[:, rim:], gap, turned[:, :rim]], axis=1)


def shards(
    science,
    template,
    owner_map,
    covering,
    row_shift,
    col_shift,
    basis_cols,
    basis_rows,
    coeffs,
    psf_kernel,
):
    image_rows, image_cols = science.shape
    devices = lax.axis_size("visit")
    position = lax.axis_index("visit")
    held_piece = (position + 1) % devices
    visit_id = held_piece // PIECES
    slot_count = covering.shape[1]
    rim = basis_cols.shape[1] // 2
    psf_rim = psf_kernel.shape[0] // 2
    blocks = image_cols // LANES
    vmem = pl.BlockSpec(memory_space=pltpu.VMEM)
    smem = pl.BlockSpec(memory_space=pltpu.SMEM)
    in_hbm = pl.BlockSpec(memory_space=pltpu.HBM)

    pieces = gather_pieces(template)

    coeff_row = lax.dynamic_index_in_dim(coeffs, visit_id, 0, keepdims=False)
    weights = (coeff_row[:, None] * basis_rows).astype(jnp.bfloat16)
    model_taps = jnp.einsum(
        "bs,bt->st", weights, basis_cols.astype(jnp.bfloat16), preferred_element_type=jnp.float32
    )
    psf_taps = psf_kernel.astype(jnp.bfloat16).astype(jnp.float32)
    model_chunks = (basis_rows.shape[1] + 3) // 2
    psf_chunks = (psf_kernel.shape[0] + 3) // 2
    edge = rim + psf_rim
    sent = jax.ShapeDtypeStruct((edge + 2 * psf_rim, blocks, LANES), jnp.bfloat16)
    rim_rows = jax.ShapeDtypeStruct((2 * psf_rim, blocks, LANES), jnp.bfloat16)
    turned_shape = jax.ShapeDtypeStruct((image_rows * blocks, LANES), jnp.float32)
    table, model_bands, psf_bands, first_rows, last_rows, turned, own = pl.pallas_call(
        prepare_kernel,
        out_shape=(
            jax.ShapeDtypeStruct((1, 3 * (slot_count + 1)), jnp.int32),
            jax.ShapeDtypeStruct((2, model_chunks, 256, 256), jnp.bfloat16),
            jax.ShapeDtypeStruct((2, psf_chunks, 256, 256), jnp.bfloat16),
            rim_rows,
            rim_rows,
            turned_shape,
            turned_shape,
        ),
        in_specs=[in_hbm] * 4 + [vmem] * 2 + [in_hbm] * 2,
        out_specs=(smem,) + (vmem,) * 6,
        scratch_shapes=[
            pltpu.SMEM(covering.shape, jnp.int32),
            pltpu.SMEM(owner_map.shape, jnp.int32),
            pltpu.SMEM(row_shift.shape, jnp.int32),
            pltpu.SMEM(col_shift.shape, jnp.int32),
            pltpu.VMEM(science.shape, science.dtype),
            pltpu.VMEM(template.shape, template.dtype),
            pltpu.SemaphoreType.DMA((6,)),
        ],
        compiler_params=pltpu.CompilerParams(vmem_limit_bytes=16 * 2**20),
        cost_estimate=cost(4),
        name="prepare",
    )(
        covering, owner_map, row_shift, col_shift,
        tap_rows(model_taps, LANES), tap_rows(psf_taps, LANES), science, template,
    )

    moved_rows = (2 * image_rows + 3) * blocks
    canvas_shape = jax.ShapeDtypeStruct((image_rows, blocks, LANES), jnp.float32)
    moved = pltpu.VMEM((moved_rows, LANES), jnp.float32)
    partial, recip = pl.pallas_call(
        near_kernel,
        out_shape=(canvas_shape, canvas_shape),
        in_specs=[smem] + [vmem] * 5,
        out_specs=(vmem, vmem),
        scratch_shapes=[
            pltpu.VMEM((slot_count - 1, moved_rows, LANES), jnp.float32),
        ],
        compiler_params=pltpu.CompilerParams(vmem_limit_bytes=20 * 2**20),
        cost_estimate=cost(11),
        name="near",
    )(table, own, *pieces[1:5])
    partial = pl.pallas_call(
        relayed_kernel,
        out_shape=canvas_shape,
        in_specs=[smem] + [vmem] * 2,
        out_specs=vmem,
        scratch_shapes=[moved],
        compiler_params=pltpu.CompilerParams(vmem_limit_bytes=12 * 2**20),
        cost_estimate=cost(5),
        name="relayed",
    )(table, partial, pieces[5])
    canvas, to_inner, to_outer = pl.pallas_call(
        canvas_kernel,
        out_shape=(turned_shape, sent, sent),
        in_specs=[smem] + [vmem] * 5,
        out_specs=(vmem, vmem, vmem),
        scratch_shapes=[moved],
        compiler_params=pltpu.CompilerParams(vmem_limit_bytes=12 * 2**20),
        cost_estimate=cost(5),
        name="canvas",
    )(table, partial, pieces[6], recip, first_rows, last_rows)

    groups = [[(first + i - 1) % devices for i in range(PIECES)] for first in range(0, devices, PIECES)]

    def swap(value, pairs):
        return lax.ppermute(value, "visit", [(g[a], g[b]) for g in groups for a, b in pairs])

    inner_rows = swap(to_inner, [(1, 2), (2, 1)])
    outer_rows = swap(to_outer, [(0, 1), (1, 0), (2, 3), (3, 2)])

    square_shape = jax.ShapeDtypeStruct((8, LANES), jnp.float32)
    inside, inside_response, inside_square = pl.pallas_call(
        lambda *refs: interior_kernel(rim, psf_rim, *refs),
        out_shape=(turned_shape, turned_shape, square_shape),
        in_specs=[vmem] * 4,
        out_specs=(vmem, vmem, vmem),
        scratch_shapes=[
            pltpu.VMEM((2, 2, 2, (image_rows // 8 + 2) * 16, 256), jnp.bfloat16),
            pltpu.VMEM((2, 2, 2, (image_rows // 8 + 2) * 16, 256), jnp.bfloat16),
        ],
        compiler_params=pltpu.CompilerParams(vmem_limit_bytes=20 * 2**20),
        cost_estimate=cost(12),
        name="interior",
    )(canvas, turned, model_bands, psf_bands)
    end_shape = jax.ShapeDtypeStruct((EDGE * blocks, LANES), jnp.float32)
    top, bottom, square = pl.pallas_call(
        lambda *refs: edge_kernel(rim, psf_rim, *refs),
        out_shape=(end_shape, end_shape, square_shape),
        in_specs=[vmem] * 6,
        out_specs=(vmem, vmem, vmem),
        scratch_shapes=[
            pltpu.VMEM(((2 * (EDGE + 2 * rim + 3) + 2 * psf_rim) * blocks, LANES), jnp.float32),
            pltpu.VMEM((2, 2, 2, (EDGE // 4 + model_chunks) * 16, 256), jnp.bfloat16),
        ],
        compiler_params=pltpu.CompilerParams(vmem_limit_bytes=16 * 2**20),
        cost_estimate=cost(4),
        name="edge",
    )(canvas, inner_rows, outer_rows, turned, model_bands, inside_square)

    totals = [square]
    for turn in SUMS:
        if isinstance(turn, int):
            links = [(g[i], g[(i + turn) % PIECES]) for g in groups for i in range(PIECES)]
        else:
            links = [(g[a], g[b]) for g in groups for p in turn for a, b in (p, p[::-1])]
        totals.append(lax.ppermute(square, "visit", links))

    difference, ends = pl.pallas_call(
        lambda *refs: rest_kernel(psf_rim, *refs),
        out_shape=(
            jax.ShapeDtypeStruct((image_rows, image_cols), jnp.float32),
            jax.ShapeDtypeStruct((2 * EDGE * blocks, LANES), jnp.float32),
        ),
        in_specs=[vmem] * 4,
        out_specs=(vmem, vmem),
        scratch_shapes=[
            pltpu.VMEM((2 * (EDGE + 2 * psf_rim + 3) * blocks, LANES), jnp.float32),
            pltpu.VMEM((2, 2, 2, (EDGE // 4 + psf_chunks) * 16, 256), jnp.bfloat16),
        ],
        compiler_params=pltpu.CompilerParams(vmem_limit_bytes=12 * 2**20),
        cost_estimate=cost(5),
        name="rest",
    )(top, bottom, inside, psf_bands)
    count = float(PIECES * image_rows * image_cols)
    detection = pl.pallas_call(
        lambda *refs: detection_kernel(count, *refs),
        out_shape=jax.ShapeDtypeStruct((image_rows, image_cols), jnp.float32),
        in_specs=[vmem] * (2 + PIECES),
        out_specs=vmem,
        compiler_params=pltpu.CompilerParams(vmem_limit_bytes=8 * 2**20),
        cost_estimate=cost(4),
        name="detection",
    )(inside_response, ends, *totals)
    return (difference, detection)


def solution(mesh):
    return jax.shard_map(
        shards,
        mesh=mesh,
        in_specs=(
            P(("groups", "visit"), None),
            P(("groups", "visit"), None),
            P("groups"),
            P(("groups", "visit"), None),
            P(("groups", "visit"), None),
            P(("groups", "visit"), None),
            P(),
            P(),
            P("groups", None),
            P(),
        ),
        out_specs=(P(("groups", "visit"), None), P(("groups", "visit"), None)),
        check_vma=False,
    )
```

time: 55.7 us -> 61.5 us (1.10)
  local copies, waits for them, and re-layouts: 0.65 us -> 5.5 us
  starting transfers between devices: 19 us -> 18 us
  matrix products: 0.25 us -> 0.97 us
  other arithmetic: 0.16 us -> 0.86 us
    unnamed x20 -> x14, local copies, waits for them, and re-layouts: 0.06 us -> 4.9 us
    ppermute x3, waiting for transfers between devices: 0.01 us -> 3.35 us  [shards(): totals.append(lax.ppermute(square, 'visit', links))]
    ppermute x2, waiting for transfers between devices: 2.79 us -> 0.01 us  [swap(): lax.ppermute(value, 'visit', [(g[a], g[b]) for g in groups for a, b in pa...]
    ppermute x6, starting transfers between devices: 9.23 us -> 8.25 us  [move(): return lax.ppermute(value, 'visit', kept)]
    pallas_call x5 -> x6, Pallas kernels: 8.5 us -> 9.26 us  [the longest x1 2.99 us: shards(): pl.pallas_call(lambda *refs: interior_kernel(rim, psf_rim, *refs), out_sh...]
    pallas_call x1, Pallas kernels: 5.29 us -> 4.56 us  [shards(): pl.pallas_call(near_kernel, out_shape=(canvas_shape, canvas_shape), in_sp...]
    dot_general x1, matrix products: 0.25 us -> 0.97 us  [shards(): jnp.einsum('bs,bt->st', weights, basis_cols.astype(jnp.bfloat16), preferr...]
    convert_element_type x1, other arithmetic: 0.01 us -> 0.7 us  [shards(): psf_taps = psf_kernel.astype(jnp.bfloat16).astype(jnp.float32)]
  transfers between devices with their start and end apart: 11 -> 11, of which waited for: 3 -> 3; matrix products, arithmetic and copies ran while one was open for 2% -> 4% of each run, Pallas kernels for 17% -> 20%
where the time goes in v1:
time: 61.5 us; the launch traced here: 61.1 us
  waiting for transfers between devices  19.9 us (32%)
  starting transfers between devices  18 us (29%)
  Pallas kernels  15 us (24%)
  local copies, waits for them, and re-layouts  5.5 us (9%)
  matrix products  0.97 us (2%)
  other arithmetic  0.86 us (1%)
  between operations  0.81 us (1%)
    ppermute x6, waiting for transfers between devices, move(): return lax.ppermute(value, 'visit', kept)  16.6 us
    ppermute x6, starting transfers between devices, move(): return lax.ppermute(value, 'visit', kept)  8.25 us
    ppermute x2, starting transfers between devices, swap(): lax.ppermute(value, 'visit', [(g[a], g[b]) for g in groups for a, b in pa...  5.18 us
    unnamed x14, local copies, waits for them, and re-layouts  4.9 us
    ppermute x3, starting transfers between devices, shards(): totals.append(lax.ppermute(square, 'visit', links))  4.62 us
    pallas_call x1, Pallas kernels, shards(): pl.pallas_call(near_kernel, out_shape=(canvas_shape, canvas_shape), in_sp...  4.56 us
    ppermute x3, waiting for transfers between devices, shards(): totals.append(lax.ppermute(square, 'visit', links))  3.35 us
    pallas_call x1, Pallas kernels, shards(): pl.pallas_call(lambda *refs: interior_kernel(rim, psf_rim, *refs), out_sh...  2.99 us
  transfers between devices with their start and end apart: 11, of which 3 were waited for; matrix products, arithmetic and copies ran while one was open for 4% of the time, Pallas kernels for 20%

profile of v1, /device:TPU:0, one launch (start us, length us, event | category | flops | bytes accessed | tf_op | source)
XLA Modules:
  0.0 61.1 jit_solution(6683143319327017895)
XLA Ops:
  0.6 0.0 copy-start
  0.6 3.1 %collective-permute-start.1 = (bf16[256,1024]{1,0:T(8,128)(2,1)}, bf16[256,1024]{1,0:T(8,128)(2,1)S(1)}, u32[]{:S(2)}, u32[]{:S(2)}) collective-permute-start(bf16[256,1024]{1,0:T(8,128)(2,1)} %piece_in.1), channel_id=1, source_target_pairs={{0,2},{1,3},{2,0},{3,1},{4,6},{5,7},{6,4},{7,5},{8,10},{9,11},{10,... | collective-permute-start | bytes 1572872 | tf_op jit(solution)/shard_map/ppermute | solution.py:43
  3.7 0.7 %collective-permute-start.3 = (bf16[256,1024]{1,0:T(8,128)(2,1)}, bf16[256,1024]{1,0:T(8,128)(2,1)S(1)}, u32[]{:S(2)}, u32[]{:S(2)}) collective-permute-start(bf16[256,1024]{1,0:T(8,128)(2,1)} %piece_in.1), channel_id=1, source_target_pairs={{1,4},{3,6},{4,1},{5,8},{6,3},{7,10},{8,5},{9,12},{10,7},{11,14},{... | collective-permute-start | bytes 1572872 | tf_op jit(solution)/shard_map/ppermute | solution.py:43
  4.4 11.4 %collective-permute-done.1.refs_1_.pair = bf16[256,1024]{1,0:T(8,128)(2,1)S(1)} collective-permute-done((bf16[256,1024]{1,0:T(8,128)(2,1)}, bf16[256,1024]{1,0:T(8,128)(2,1)S(1)}, u32[]{:S(2)}, u32[]{:S(2)}) %collective-permute-start.1) | collective-permute-done | bytes 524320 | tf_op jit(solution)/shard_map/ppermute | solution.py:43
  15.8 0.0 collective-permute-done.3.refs_3_.far
  15.9 3.7 %collective-permute-start.4 = (bf16[256,1024]{1,0:T(8,128)(2,1)S(1)}, bf16[256,1024]{1,0:T(8,128)(2,1)S(1)}, u32[]{:S(2)}, u32[]{:S(2)}) collective-permute-start(bf16[256,1024]{1,0:T(8,128)(2,1)S(1)} %relay.1), channel_id=1, source_target_pairs={{0,4},{1,2},{2,1},{4,8},{5,6},{6,5},{7,3},{8,12},{9,10},{10,9},{11... | collective-permute-start | bytes 1572872 | tf_op jit(solution)/shard_map/ppermute | solution.py:43
  19.6 0.1 collective-permute-start
  19.7 0.0 copy-done
  19.8 1.0 %fusion = f32[21,21]{1,0:T(8,128)S(1)} fusion(f32[20,21]{1,0:T(8,128)} %param.17, f32[20,21]{1,0:T(8,128)} %param.16, f32[20]{0:T(128)S(1)} %dynamic-slice_bitcast_fusion), kind=kOutput, calls=%fused_computation.3 | convolution fusion | flops 18900 | bytes 5204 | tf_op jit(solution)/shard_map/bs,bt->st/dot_general | solution.py:535
  20.7 0.4 collective-permute-start.2
  21.2 5.1 %collective-permute-done.4.piece = bf16[256,1024]{1,0:T(8,128)(2,1)S(1)} collective-permute-done((bf16[256,1024]{1,0:T(8,128)(2,1)S(1)}, bf16[256,1024]{1,0:T(8,128)(2,1)S(1)}, u32[]{:S(2)}, u32[]{:S(2)}) %collective-permute-start.4) | collective-permute-done | bytes 524320 | tf_op jit(solution)/shard_map/ppermute | solution.py:43
  26.3 0.2 collective-permute-start.5
  26.5 0.7 %convert_convert_fusion = f32[9,9]{1,0:T(8,128)S(1)} fusion(f32[9,9]{1,0:T(8,128)} %param.19), kind=kLoop, calls=%fused_computation.6 | loop fusion | flops 162 | bytes 648 | tf_op jit(solution)/shard_map/convert_element_type | solution.py:538
  27.2 0.1 slice.33
  27.3 0.1 slice.27
  27.4 0.1 slice.25
  27.4 0.1 slice.35
  27.5 0.1 slice.31
  27.6 0.1 slice.29
  27.6 0.1 pad.4.clone
  27.7 0.1 pad.1.clone
  27.8 0.1 pad_maximum_fusion.1.psf_taps
  27.9 0.1 pad_maximum_fusion.model_taps
  28.0 0.0 copy-start.1
  28.0 1.2 %copy-done.1 = f32[256,1024]{1,0:T(8,128)S(1)} copy-done((f32[256,1024]{1,0:T(8,128)S(1)}, f32[256,1024]{1,0:T(8,128)}, u32[]{:S(2)}) %copy-start.1) | copy-done | bytes 1048600
  29.2 0.0 copy-start.2
  29.2 1.0 %copy-done.2 = bf16[256,1024]{1,0:T(8,128)(2,1)S(1)} copy-done((bf16[256,1024]{1,0:T(8,128)(2,1)S(1)}, bf16[256,1024]{1,0:T(8,128)(2,1)}, u32[]{:S(2)}) %copy-start.2) | copy-done | bytes 524312
  30.2 0.0 copy-start.3
  30.2 0.7 %copy-done.3 = s32[1,4]{1,0:T(1,128)S(1)} copy-done((s32[1,4]{1,0:T(1,128)S(1)}, s32[1,4]{1,0:T(1,128)}, u32[]{:S(2)}) %copy-start.3) | copy-done | bytes 40
  30.9 0.0 copy-start.4
  30.9 0.7 %copy-done.4 = s32[16]{0:T(128)S(1)} copy-done((s32[16]{0:T(128)S(1)}, s32[16]{0:T(128)}, u32[]{:S(2)}) %copy-start.4) | copy-done | bytes 88
  31.6 0.0 copy-start.5
  31.6 0.7 %copy-done.5 = s32[1,4]{1,0:T(1,128)S(1)} copy-done((s32[1,4]{1,0:T(1,128)S(1)}, s32[1,4]{1,0:T(1,128)}, u32[]{:S(2)}) %copy-start.5) | copy-done | bytes 40
  32.2 0.0 copy-start.6
  32.2 0.7 %copy-done.6 = s32[1,4]{1,0:T(1,128)S(1)} copy-done((s32[1,4]{1,0:T(1,128)S(1)}, s32[1,4]{1,0:T(1,128)}, u32[]{:S(2)}) %copy-start.6) | copy-done | bytes 40
  32.9 2.2 %prepare.1 = (s32[1,15]{1,0:T(1,128)S(1)}, bf16[2,12,256,256]{3,2,1,0:T(8,128)(2,1)S(1)}, bf16[2,6,256,256]{3,2,1,0:T(8,128)(2,1)S(1)}, bf16[8,8,128]{2,1,0:T(8,...) custom-call(s32[1,4]{1,0:T(1,128)S(1)} %copy-done.3, ...), custom_call_target="tpu_custom_call" | custom-call | bytes 4194304 | tf_op jit(solution)/shard_map/prepare/pallas_call | solution.py:545
  35.1 0.0 collective-permute-done.refs_0_
  35.1 0.0 collective-permute-done.2.refs_2_
  35.1 4.6 %near.1 = (f32[256,8,128]{2,1,0:T(8,128)S(1)}, f32[256,8,128]{2,1,0:T(8,128)S(1)}) custom-call(s32[1,15]{1,0:T(1,128)S(1)} %get-tuple-element.22.table, f32[2048,128]{1,0:T(8,128)S(1)} %get-tuple-element.23.own, bf16[256,1024]{1,0:T(8,128)(2,1)S(1)} %collective-permute-done.refs_0_, bf16[256,1024]{1,0:T(8,128)(2,1)S(1)} %collective-permute-done.1.refs_1_.pair, ...), custom_call_target="tpu_custom_call" | custom-call | bytes 11534336 | tf_op jit(solution)/shard_map/near/pallas_call | solution.py:578
  39.7 0.7 %relayed.1.partial = f32[256,8,128]{2,1,0:T(8,128)S(1)} custom-call(s32[1,15]{1,0:T(1,128)S(1)} %get-tuple-element.22.table, f32[256,8,128]{2,1,0:T(8,128)S(1)} %get-tuple-element.24.partial, bf16[256,1024]{1,0:T(8,128)(2,1)S(1)} %collective-permute-done.4.piece), custom_call_target="tpu_custom_call" | custom-call | bytes 5242880 | tf_op jit(solution)/shard_map/relayed/pallas_call | solution.py:590
  40.4 0.0 collective-permute-done.5.piece
  40.4 0.9 %canvas.1 = (f32[2048,128]{1,0:T(8,128)S(1)}, bf16[22,8,128]{2,1,0:T(8,128)(2,1)S(1)}, bf16[22,8,128]{2,1,0:T(8,128)(2,1)S(1)}) custom-call(s32[1,15]{1,0:T(1,128)S(1)} %get-tuple-element.22.table, f32[256,8,128]{2,1,0:T(8,128)S(1)} %relayed.1.partial, bf16[256,1024]{1,0:T(8,128)(2,1)S(1)} %collective-permute-done.5.piece, ...), custom_call_target="tpu_custom_call" | custom-call | bytes 5242880 | tf_op jit(solution)/shard_map/canvas/pallas_call | solution.py:600
  41.3 1.9 %collective-permute-start.6 = (bf16[22,8,128]{2,1,0:T(8,128)(2,1)S(1)}, bf16[22,8,128]{2,1,0:T(8,128)(2,1)S(1)}, u32[]{:S(2)}, u32[]{:S(2)}) collective-permute-start(bf16[22,8,128]{2,1,0:T(8,128)(2,1)S(1)} %get-tuple-element.29), channel_id=1, source_target_pairs={{0,1},{1,0},{4,5},{5,4},{8,9},{9,8},{12,13},{13,12},{16,17},{17,16... | collective-permute-start | bytes 135176 | tf_op jit(solution)/shard_map/ppermute | solution.py:614
  43.3 3.2 %collective-permute-start.7 = (bf16[22,8,128]{2,1,0:T(8,128)(2,1)S(1)}, bf16[22,8,128]{2,1,0:T(8,128)(2,1)S(1)}, u32[]{:S(2)}, u32[]{:S(2)}) collective-permute-start(bf16[22,8,128]{2,1,0:T(8,128)(2,1)S(1)} %get-tuple-element.30), channel_id=1, source_target_pairs={{15,0},{0,15},{1,2},{2,1},{3,4},{4,3},{5,6},{6,5},{7,8},{8,7},{9,1... | collective-permute-start | bytes 135176 | tf_op jit(solution)/shard_map/ppermute | solution.py:614
  46.5 3.0 %interior.1 = (f32[2048,128]{1,0:T(8,128)S(1)}, f32[2048,128]{1,0:T(8,128)S(1)}, f32[8,128]{1,0:T(8,128)S(1)}) custom-call(f32[2048,128]{1,0:T(8,128)S(1)} %get-tuple-element.28.refs_0_, f32[2048,128]{1,0:T(8,128)S(1)} %get-tuple-element.31.refs_1_.refs_3_, bf16[2,12,256,256]{3,2,1,0:T(8,128)(2,1)S(1)} %get-tuple-element.32.refs_2_.refs_4_, ...), custom_call_target="tpu_custom_call" | custom-call | bytes 12582912 | tf_op jit(solution)/shard_map/interior/pallas_call | solution.py:620
  49.5 0.0 collective-permute-done.6.refs_1_
  49.5 0.0 collective-permute-done.7.refs_2_
  49.5 0.9 %edge.1 = (f32[128,128]{1,0:T(8,128)S(1)}, f32[128,128]{1,0:T(8,128)S(1)}, f32[8,128]{1,0:T(8,128)S(1)}) custom-call(f32[2048,128]{1,0:T(8,128)S(1)} %get-tuple-element.28.refs_0_, bf16[22,8,128]{2,1,0:T(8,128)(2,1)S(1)} %collective-permute-done.6.refs_1_, bf16[22,8,128]{2,1,0:T(8,128)(2,1)S(1)} %collective-permute-done.7.refs_2_, ...), custom_call_target="tpu_custom_call" | custom-call | bytes 4194304 | tf_op jit(solution)/shard_map/edge/pallas_call | solution.py:634
  50.4 0.1 collective-permute-start.10
  50.5 3.7 %collective-permute-start.8 = (f32[8,128]{1,0:T(8,128)S(1)}, f32[8,128]{1,0:T(8,128)S(1)}, u32[]{:S(2)}, u32[]{:S(2)}) collective-permute-start(f32[8,128]{1,0:T(8,128)S(1)} %get-tuple-element.41.refs_2_), channel_id=1, source_target_pairs={{15,1},{1,15},{0,2},{2,0},{3,5},{5,3},{4,6},{6,4},{7,9},{9,7},{8,1... | collective-permute-start | bytes 12296 | tf_op jit(solution)/shard_map/ppermute | solution.py:654
  54.2 0.8 %collective-permute-start.9 = (f32[8,128]{1,0:T(8,128)S(1)}, f32[8,128]{1,0:T(8,128)S(1)}, u32[]{:S(2)}, u32[]{:S(2)}) collective-permute-start(f32[8,128]{1,0:T(8,128)S(1)} %get-tuple-element.41.refs_2_), channel_id=1, source_target_pairs={{15,0},{0,15},{1,2},{2,1},{3,4},{4,3},{5,6},{6,5},{7,8},{8,7},{9,1... | collective-permute-start | bytes 12296 | tf_op jit(solution)/shard_map/ppermute | solution.py:654
  55.1 1.5 %rest.1 = (f32[256,1024]{1,0:T(8,128)}, f32[256,128]{1,0:T(8,128)S(1)}) custom-call(f32[128,128]{1,0:T(8,128)S(1)} %get-tuple-element.35.refs_0_, f32[128,128]{1,0:T(8,128)S(1)} %get-tuple-element.36.refs_1_, f32[2048,128]{1,0:T(8,128)S(1)} %get-tuple-element.37.refs_2_, bf16[2,6,256,256]{3,2,1,0:T(8,128)(2,1)S(1)} %get-tuple-element.33.refs_3_), custom_call_target="tpu_custom_call" | custom-call | bytes 5242880 | tf_op jit(solution)/shard_map/rest/pallas_call | solution.py:656
  56.6 0.0 collective-permute-done.10.refs_5_
  56.6 0.0 collective-permute-done.8.refs_3_
  56.6 3.3 %collective-permute-done.9.refs_4_ = f32[8,128]{1,0:T(8,128)S(1)} collective-permute-done((f32[8,128]{1,0:T(8,128)S(1)}, f32[8,128]{1,0:T(8,128)S(1)}, u32[]{:S(2)}, u32[]{:S(2)}) %collective-permute-start.9) | collective-permute-done | bytes 4128 | tf_op jit(solution)/shard_map/ppermute | solution.py:654
  59.9 1.2 %detection.1 = f32[256,1024]{1,0:T(8,128)} custom-call(f32[2048,128]{1,0:T(8,128)S(1)} %get-tuple-element.39.refs_0_, f32[256,128]{1,0:T(8,128)S(1)} %get-tuple-element.40.refs_1_, f32[8,128]{1,0:T(8,128)S(1)} %get-tuple-element.41.refs_2_, f32[8,128]{1,0:T(8,128)S(1)} %collective-permute-done.8.refs_3_, f32[8,128]{1,0:T(8,128)S(1)} %collective-permute-done.9.refs_4_, ...), custom_call_target="tpu_custom_call" | custom-call | bytes 4194304 | tf_op jit(solution)/shard_map/detection/pallas_call | solution.py:673
  (4 shorter events, 0.0 us)
Async XLA Ops:
  0.6 19.1 %copy-start = (f32[4,20]{1,0:T(4,128)S(1)}, f32[4,20]{1,0:T(4,128)}, u32[]{:S(2)}) copy-start(f32[4,20]{1,0:T(4,128)} %param.18) | copy-start | bytes 964
  0.6 15.2 %collective-permute-start.1 = (bf16[256,1024]{1,0:T(8,128)(2,1)}, bf16[256,1024]{1,0:T(8,128)(2,1)S(1)}, u32[]{:S(2)}, u32[]{:S(2)}) collective-permute-start(bf16[256,1024]{1,0:T(8,128)(2,1)} %piece_in.1), channel_id=1, source_target_pairs={{0,2},{1,3},{2,0},{3,1},{4,6},{5,7},{6,4},{7,5},{8,10},{9,11},{10,... | collective-permute-start | bytes 1572872 | tf_op jit(solution)/shard_map/ppermute | solution.py:43
  3.7 12.1 %collective-permute-start.3 = (bf16[256,1024]{1,0:T(8,128)(2,1)}, bf16[256,1024]{1,0:T(8,128)(2,1)S(1)}, u32[]{:S(2)}, u32[]{:S(2)}) collective-permute-start(bf16[256,1024]{1,0:T(8,128)(2,1)} %piece_in.1), channel_id=1, source_target_pairs={{1,4},{3,6},{4,1},{5,8},{6,3},{7,10},{8,5},{9,12},{10,7},{11,14},{... | collective-permute-start | bytes 1572872 | tf_op jit(solution)/shard_map/ppermute | solution.py:43
  15.9 10.4 %collective-permute-start.4 = (bf16[256,1024]{1,0:T(8,128)(2,1)S(1)}, bf16[256,1024]{1,0:T(8,128)(2,1)S(1)}, u32[]{:S(2)}, u32[]{:S(2)}) collective-permute-start(bf16[256,1024]{1,0:T(8,128)(2,1)S(1)} %relay.1), channel_id=1, source_target_pairs={{0,4},{1,2},{2,1},{4,8},{5,6},{6,5},{7,3},{8,12},{9,10},{10,9},{11... | collective-permute-start | bytes 1572872 | tf_op jit(solution)/shard_map/ppermute | solution.py:43
  19.6 15.5 %collective-permute-start = (bf16[256,1024]{1,0:T(8,128)(2,1)}, bf16[256,1024]{1,0:T(8,128)(2,1)S(1)}, u32[]{:S(2)}, u32[]{:S(2)}) collective-permute-start(bf16[256,1024]{1,0:T(8,128)(2,1)} %piece_in.1), channel_id=1, source_target_pairs={{0,1},{1,0},{2,3},{3,2},{4,5},{5,4},{6,7},{7,6},{8,9},{9,8},{10,11... | collective-permute-start | bytes 1572872 | tf_op jit(solution)/shard_map/ppermute | solution.py:43
  20.7 14.4 %collective-permute-start.2 = (bf16[256,1024]{1,0:T(8,128)(2,1)S(1)}, bf16[256,1024]{1,0:T(8,128)(2,1)S(1)}, u32[]{:S(2)}, u32[]{:S(2)}) collective-permute-start(bf16[256,1024]{1,0:T(8,128)(2,1)S(1)} %collective-permute-done.1.refs_1_.pair), channel_id=1, source_target_pairs={{0,1},{1,0},{2,3},{3,2},{4,5},{5,4},{6,7},{7,6},{8,9},{9,8},{10,11... | collective-permute-start | bytes 1572872 | tf_op jit(solution)/shard_map/ppermute | solution.py:43
  26.3 14.1 %collective-permute-start.5 = (bf16[256,1024]{1,0:T(8,128)(2,1)S(1)}, bf16[256,1024]{1,0:T(8,128)(2,1)S(1)}, u32[]{:S(2)}, u32[]{:S(2)}) collective-permute-start(bf16[256,1024]{1,0:T(8,128)(2,1)S(1)} %collective-permute-done.4.piece), channel_id=1, source_target_pairs={{0,1},{1,0},{2,3},{3,2},{4,5},{5,4},{6,7},{7,6},{8,9},{9,8},{10,11... | collective-permute-start | bytes 1572872 | tf_op jit(solution)/shard_map/ppermute | solution.py:43
  28.0 1.2 %copy-start.1 = (f32[256,1024]{1,0:T(8,128)S(1)}, f32[256,1024]{1,0:T(8,128)}, u32[]{:S(2)}) copy-start(f32[256,1024]{1,0:T(8,128)} %science_in.1) | copy-start | bytes 3145732
  29.2 1.0 %copy-start.2 = (bf16[256,1024]{1,0:T(8,128)(2,1)S(1)}, bf16[256,1024]{1,0:T(8,128)(2,1)}, u32[]{:S(2)}) copy-start(bf16[256,1024]{1,0:T(8,128)(2,1)} %piece_in.1) | copy-start | bytes 1572868
  30.2 0.7 %copy-start.3 = (s32[1,4]{1,0:T(1,128)S(1)}, s32[1,4]{1,0:T(1,128)}, u32[]{:S(2)}) copy-start(s32[1,4]{1,0:T(1,128)} %covering_in.1) | copy-start | bytes 52
  30.9 0.7 %copy-start.4 = (s32[16]{0:T(128)S(1)}, s32[16]{0:T(128)}, u32[]{:S(2)}) copy-start(s32[16]{0:T(128)} %owner_in.1) | copy-start | bytes 196
  31.6 0.7 %copy-start.5 = (s32[1,4]{1,0:T(1,128)S(1)}, s32[1,4]{1,0:T(1,128)}, u32[]{:S(2)}) copy-start(s32[1,4]{1,0:T(1,128)} %row_in.1) | copy-start | bytes 52
  32.2 0.7 %copy-start.6 = (s32[1,4]{1,0:T(1,128)S(1)}, s32[1,4]{1,0:T(1,128)}, u32[]{:S(2)}) copy-start(s32[1,4]{1,0:T(1,128)} %col_in.1) | copy-start | bytes 52
  41.3 8.2 %collective-permute-start.6 = (bf16[22,8,128]{2,1,0:T(8,128)(2,1)S(1)}, bf16[22,8,128]{2,1,0:T(8,128)(2,1)S(1)}, u32[]{:S(2)}, u32[]{:S(2)}) collective-permute-start(bf16[22,8,128]{2,1,0:T(8,128)(2,1)S(1)} %get-tuple-element.29), channel_id=1, source_target_pairs={{0,1},{1,0},{4,5},{5,4},{8,9},{9,8},{12,13},{13,12},{16,17},{17,16... | collective-permute-start | bytes 135176 | tf_op jit(solution)/shard_map/ppermute | solution.py:614
  43.3 6.2 %collective-permute-start.7 = (bf16[22,8,128]{2,1,0:T(8,128)(2,1)S(1)}, bf16[22,8,128]{2,1,0:T(8,128)(2,1)S(1)}, u32[]{:S(2)}, u32[]{:S(2)}) collective-permute-start(bf16[22,8,128]{2,1,0:T(8,128)(2,1)S(1)} %get-tuple-element.30), channel_id=1, source_target_pairs={{15,0},{0,15},{1,2},{2,1},{3,4},{4,3},{5,6},{6,5},{7,8},{8,7},{9,1... | collective-permute-start | bytes 135176 | tf_op jit(solution)/shard_map/ppermute | solution.py:614
  50.4 6.2 %collective-permute-start.10 = (f32[8,128]{1,0:T(8,128)S(1)}, f32[8,128]{1,0:T(8,128)S(1)}, u32[]{:S(2)}, u32[]{:S(2)}) collective-permute-start(f32[8,128]{1,0:T(8,128)S(1)} %get-tuple-element.41.refs_2_), channel_id=1, source_target_pairs={{15,2},{2,15},{0,1},{1,0},{3,6},{6,3},{4,5},{5,4},{7,10},{10,7},{8... | collective-permute-start | bytes 12296 | tf_op jit(solution)/shard_map/ppermute | solution.py:654
  50.5 6.1 %collective-permute-start.8 = (f32[8,128]{1,0:T(8,128)S(1)}, f32[8,128]{1,0:T(8,128)S(1)}, u32[]{:S(2)}, u32[]{:S(2)}) collective-permute-start(f32[8,128]{1,0:T(8,128)S(1)} %get-tuple-element.41.refs_2_), channel_id=1, source_target_pairs={{15,1},{1,15},{0,2},{2,0},{3,5},{5,3},{4,6},{6,4},{7,9},{9,7},{8,1... | collective-permute-start | bytes 12296 | tf_op jit(solution)/shard_map/ppermute | solution.py:654
  54.2 5.7 %collective-permute-start.9 = (f32[8,128]{1,0:T(8,128)S(1)}, f32[8,128]{1,0:T(8,128)S(1)}, u32[]{:S(2)}, u32[]{:S(2)}) collective-permute-start(f32[8,128]{1,0:T(8,128)S(1)} %get-tuple-element.41.refs_2_), channel_id=1, source_target_pairs={{15,0},{0,15},{1,2},{2,1},{3,4},{4,3},{5,6},{6,5},{7,8},{8,7},{9,1... | collective-permute-start | bytes 12296 | tf_op jit(solution)/shard_map/ppermute | solution.py:654

commit v2 on v1

--- a/solution.py
+++ b/solution.py
@@ -64,6 +64,7 @@
 
 CHUNK = 16
 EDGE = 16
+STEPS = 2
 
 
 def spread(piece, turn, target, first):
@@ -361,9 +362,7 @@
             put(4 * g + 2 * pair + 1, pltpu.roll(jnp.where(lower, b, a), LANES // 2, 1))
 
 
-def interior_kernel(
-    rim, psf_rim, canvas, science, model_bands, psf_bands, difference, response, square, packed, packed_psf,
-):
+def interior_kernel(rim, psf_rim, canvas, science, model_bands, difference, square, packed):
     blocks = 8
     rows = canvas.shape[0] // blocks
     first = EDGE - psf_rim
@@ -379,13 +378,6 @@
 
     unfold(packed, model_bands, [(0, groups)], put)
     square[...] = (totals[0] + totals[1]) + (totals[2] + totals[3])
-    groups = (rows - 2 * EDGE) // 4
-    pack_rows(difference, first * blocks, groups + psf_bands.shape[1] // 2 - 1, packed_psf, 0)
-
-    def put_response(i, value):
-        response[(EDGE + i) * blocks : (EDGE + i + 1) * blocks, :] = value
-
-    unfold(packed_psf, psf_bands, [(0, groups)], put_response)
 
 
 def edge_kernel(
@@ -446,38 +438,27 @@
 def rest_kernel(psf_rim, top, bottom, inside, bands, difference, response, joint, packed):
     blocks = 8
     rows, _ = difference.shape
-    groups = EDGE // 4
-    span = EDGE + 2 * psf_rim
-    more = span - EDGE
-    starts = (blocks, (span + 3) * blocks)
-    joint[starts[0] : starts[0] + EDGE * blocks, :] = top[...]
+    start = blocks
+    more = rows + 2 * psf_rim - 2 * EDGE
+    first = start + EDGE * blocks
+    joint[start:first, :] = top[...]
     from_row = EDGE - psf_rim
-    to = starts[0] + EDGE * blocks
-    joint[to : to + more * blocks, :] = inside[from_row * blocks : (from_row + more) * blocks, :]
-    from_row = rows - EDGE + psf_rim - more
-    joint[starts[1] : starts[1] + more * blocks, :] = inside[from_row * blocks : (from_row + more) * blocks, :]
-    joint[starts[1] + more * blocks : starts[1] + span * blocks, :] = bottom[...]
-    steps = groups + bands.shape[1] // 2 - 1
-    pairs = (steps + 1) // 2
-    pack_rows(joint, starts[0], steps, packed, 0)
-    pack_rows(joint, starts[1], steps, packed, pairs)
+    joint[first : first + more * blocks, :] = inside[from_row * blocks : (from_row + more) * blocks, :]
+    joint[first + more * blocks : first + (more + EDGE) * blocks, :] = bottom[...]
+    groups = rows // 4
+    pack_rows(joint, start, groups + bands.shape[1] // 2 - 1, packed, 0)
 
     def put(i, value):
         response[i * blocks : (i + 1) * blocks, :] = value
 
-    unfold(packed, bands, [(0, groups), (pairs, groups)], put)
+    unfold(packed, bands, [(0, groups)], put)
     for row in range(0, rows, 8):
-        if row < EDGE:
-            source, at = joint, starts[0] + (row + psf_rim) * blocks
-        elif row >= rows - EDGE:
-            source, at = joint, starts[1] + (row - (rows - EDGE - psf_rim)) * blocks
-        else:
-            source, at = inside, row * blocks
         for k in range(blocks):
-            difference[row : row + 8, k * LANES : (k + 1) * LANES] = source[pl.ds(at + k, 8, stride=blocks), :]
-
-
-def detection_kernel(count, inside, ends, *refs):
+            at = pl.ds(start + (row + psf_rim) * blocks + k, 8, stride=blocks)
+            difference[row : row + 8, k * LANES : (k + 1) * LANES] = joint[at, :]
+
+
+def detection_kernel(count, response, *refs):
     out = refs[-1]
     total = refs[0][...]
     for ref in refs[1:-1]:
@@ -485,15 +466,11 @@
     scale = 1.0 / jnp.sqrt(total / count + 1e-06)
     rows, cols = out.shape
     blocks = cols // LANES
+    first = pl.multiple_of(pl.program_id(0) * (rows * blocks), rows * blocks)
     for row in range(0, rows, 8):
-        if row < EDGE:
-            source, at = ends, row * blocks
-        elif row >= rows - EDGE:
-            source, at = ends, (row - (rows - 2 * EDGE)) * blocks
-        else:
-            source, at = inside, row * blocks
         for k in range(blocks):
-            out[row : row + 8, k * LANES : (k + 1) * LANES] = source[pl.ds(at + k, 8, stride=blocks), :] * scale
+            at = pl.ds(first + row * blocks + k, 8, stride=blocks)
+            out[row : row + 8, k * LANES : (k + 1) * LANES] = response[at, :] * scale
 
 
 def tap_rows(taps, width):
@@ -617,19 +594,16 @@
     outer_rows = swap(to_outer, [(0, 1), (1, 0), (2, 3), (3, 2)])
 
     square_shape = jax.ShapeDtypeStruct((8, LANES), jnp.float32)
-    inside, inside_response, inside_square = pl.pallas_call(
+    inside, inside_square = pl.pallas_call(
         lambda *refs: interior_kernel(rim, psf_rim, *refs),
-        out_shape=(turned_shape, turned_shape, square_shape),
-        in_specs=[vmem] * 4,
-        out_specs=(vmem, vmem, vmem),
-        scratch_shapes=[
-            pltpu.VMEM((2, 2, 2, (image_rows // 8 + 2) * 16, 256), jnp.bfloat16),
-            pltpu.VMEM((2, 2, 2, (image_rows // 8 + 2) * 16, 256), jnp.bfloat16),
-        ],
-        compiler_params=pltpu.CompilerParams(vmem_limit_bytes=20 * 2**20),
-        cost_estimate=cost(12),
+        out_shape=(turned_shape, square_shape),
+        in_specs=[vmem] * 3,
+        out_specs=(vmem, vmem),
+        scratch_shapes=[pltpu.VMEM((2, 2, 2, (image_rows // 8 + 2) * 16, 256), jnp.bfloat16)],
+        compiler_params=pltpu.CompilerParams(vmem_limit_bytes=16 * 2**20),
+        cost_estimate=cost(7),
         name="interior",
-    )(canvas, turned, model_bands, psf_bands)
+    )(canvas, turned, model_bands)
     end_shape = jax.ShapeDtypeStruct((EDGE * blocks, LANES), jnp.float32)
     top, bottom, square = pl.pallas_call(
         lambda *refs: edge_kernel(rim, psf_rim, *refs),
@@ -653,32 +627,30 @@
             links = [(g[a], g[b]) for g in groups for p in turn for a, b in (p, p[::-1])]
         totals.append(lax.ppermute(square, "visit", links))
 
-    difference, ends = pl.pallas_call(
+    difference, response = pl.pallas_call(
         lambda *refs: rest_kernel(psf_rim, *refs),
-        out_shape=(
-            jax.ShapeDtypeStruct((image_rows, image_cols), jnp.float32),
-            jax.ShapeDtypeStruct((2 * EDGE * blocks, LANES), jnp.float32),
-        ),
+        out_shape=(jax.ShapeDtypeStruct((image_rows, image_cols), jnp.float32), turned_shape),
         in_specs=[vmem] * 4,
         out_specs=(vmem, vmem),
         scratch_shapes=[
-            pltpu.VMEM((2 * (EDGE + 2 * psf_rim + 3) * blocks, LANES), jnp.float32),
-            pltpu.VMEM((2, 2, 2, (EDGE // 4 + psf_chunks) * 16, 256), jnp.bfloat16),
+            pltpu.VMEM(((image_rows + 2 * psf_rim + 3) * blocks, LANES), jnp.float32),
+            pltpu.VMEM((2, 2, 2, (image_rows // 8 + 2) * 16, 256), jnp.bfloat16),
         ],
-        compiler_params=pltpu.CompilerParams(vmem_limit_bytes=12 * 2**20),
-        cost_estimate=cost(5),
+        compiler_params=pltpu.CompilerParams(vmem_limit_bytes=16 * 2**20),
+        cost_estimate=cost(8),
         name="rest",
     )(top, bottom, inside, psf_bands)
     count = float(PIECES * image_rows * image_cols)
     detection = pl.pallas_call(
         lambda *refs: detection_kernel(count, *refs),
         out_shape=jax.ShapeDtypeStruct((image_rows, image_cols), jnp.float32),
-        in_specs=[vmem] * (2 + PIECES),
-        out_specs=vmem,
+        grid=(STEPS,),
+        in_specs=[vmem] * (1 + PIECES),
+        out_specs=pl.BlockSpec((image_rows // STEPS, image_cols), lambda i: (i, 0)),
         compiler_params=pltpu.CompilerParams(vmem_limit_bytes=8 * 2**20),
         cost_estimate=cost(4),
         name="detection",
-    )(inside_response, ends, *totals)
+    )(response, *totals)
     return (difference, detection)
 
 

time: 61.5 us -> 61.4 us (level)
  Pallas kernels: 15 us -> 14.1 us
  waiting for transfers between devices: 19.9 us -> 20.7 us
    pallas_call x1, Pallas kernels: 2.99 us -> 1.89 us  [shards(): pl.pallas_call(lambda *refs: interior_kernel(rim, psf_rim, *refs), out_sh...]
    ppermute x2, waiting for transfers between devices: 0.01 us -> 1.09 us  [swap(): lax.ppermute(value, 'visit', [(g[a], g[b]) for g in groups for a, b in pa...]
  transfers between devices with their start and end apart: 11 -> 11, of which waited for: 3 -> 4; matrix products, arithmetic and copies ran while one was open for 4% -> 4% of each run, Pallas kernels for 20% -> 19%
where the time goes in v2:
time: 61.4 us; the launch traced here: 61 us
  waiting for transfers between devices  20.7 us (34%)
  starting transfers between devices  18 us (29%)
  Pallas kernels  14.1 us (23%)
  local copies, waits for them, and re-layouts  5.5 us (9%)
  matrix products  0.97 us (2%)
  other arithmetic  0.86 us (1%)
  between operations  0.8 us (1%)
    ppermute x6, waiting for transfers between devices, move(): return lax.ppermute(value, 'visit', kept)  16.6 us
    ppermute x6, starting transfers between devices, move(): return lax.ppermute(value, 'visit', kept)  8.25 us
    ppermute x2, starting transfers between devices, swap(): lax.ppermute(value, 'visit', [(g[a], g[b]) for g in groups for a, b in pa...  5.18 us
    unnamed x14, local copies, waits for them, and re-layouts  4.9 us
    ppermute x3, starting transfers between devices, shards(): totals.append(lax.ppermute(square, 'visit', links))  4.62 us
    pallas_call x1, Pallas kernels, shards(): pl.pallas_call(near_kernel, out_shape=(canvas_shape, canvas_shape), in_sp...  4.56 us
    ppermute x3, waiting for transfers between devices, shards(): totals.append(lax.ppermute(square, 'visit', links))  3.01 us
    pallas_call x1, Pallas kernels, shards(): pl.pallas_call(prepare_kernel, out_shape=(jax.ShapeDtypeStruct((1, 3 * (s...  2.22 us
  transfers between devices with their start and end apart: 11, of which 4 were waited for; matrix products, arithmetic and copies ran while one was open for 4% of the time, Pallas kernels for 19%

profile of v2, /device:TPU:0, one launch (start us, length us, event | category | flops | bytes accessed | tf_op | source)
XLA Modules:
  0.0 61.0 jit_solution(15225134868213268285)
XLA Ops:
  0.6 0.0 copy-start
  0.6 3.1 %collective-permute-start.1 = (bf16[256,1024]{1,0:T(8,128)(2,1)}, bf16[256,1024]{1,0:T(8,128)(2,1)S(1)}, u32[]{:S(2)}, u32[]{:S(2)}) collective-permute-start(bf16[256,1024]{1,0:T(8,128)(2,1)} %piece_in.1), channel_id=1, source_target_pairs={{0,2},{1,3},{2,0},{3,1},{4,6},{5,7},{6,4},{7,5},{8,10},{9,11},{10,... | collective-permute-start | bytes 1572872 | tf_op jit(solution)/shard_map/ppermute | solution.py:43
  3.7 0.7 %collective-permute-start.3 = (bf16[256,1024]{1,0:T(8,128)(2,1)}, bf16[256,1024]{1,0:T(8,128)(2,1)S(1)}, u32[]{:S(2)}, u32[]{:S(2)}) collective-permute-start(bf16[256,1024]{1,0:T(8,128)(2,1)} %piece_in.1), channel_id=1, source_target_pairs={{1,4},{3,6},{4,1},{5,8},{6,3},{7,10},{8,5},{9,12},{10,7},{11,14},{... | collective-permute-start | bytes 1572872 | tf_op jit(solution)/shard_map/ppermute | solution.py:43
  4.4 11.4 %collective-permute-done.1.refs_1_.pair = bf16[256,1024]{1,0:T(8,128)(2,1)S(1)} collective-permute-done((bf16[256,1024]{1,0:T(8,128)(2,1)}, bf16[256,1024]{1,0:T(8,128)(2,1)S(1)}, u32[]{:S(2)}, u32[]{:S(2)}) %collective-permute-start.1) | collective-permute-done | bytes 524320 | tf_op jit(solution)/shard_map/ppermute | solution.py:43
  15.8 0.0 collective-permute-done.3.refs_3_.far
  15.9 3.7 %collective-permute-start.4 = (bf16[256,1024]{1,0:T(8,128)(2,1)S(1)}, bf16[256,1024]{1,0:T(8,128)(2,1)S(1)}, u32[]{:S(2)}, u32[]{:S(2)}) collective-permute-start(bf16[256,1024]{1,0:T(8,128)(2,1)S(1)} %relay.1), channel_id=1, source_target_pairs={{0,4},{1,2},{2,1},{4,8},{5,6},{6,5},{7,3},{8,12},{9,10},{10,9},{11... | collective-permute-start | bytes 1572872 | tf_op jit(solution)/shard_map/ppermute | solution.py:43
  19.6 0.1 collective-permute-start
  19.7 0.0 copy-done
  19.8 1.0 %fusion = f32[21,21]{1,0:T(8,128)S(1)} fusion(f32[20,21]{1,0:T(8,128)} %param.17, f32[20,21]{1,0:T(8,128)} %param.16, f32[20]{0:T(128)S(1)} %dynamic-slice_bitcast_fusion), kind=kOutput, calls=%fused_computation.3 | convolution fusion | flops 18900 | bytes 5204 | tf_op jit(solution)/shard_map/bs,bt->st/dot_general | solution.py:512
  20.7 0.4 collective-permute-start.2
  21.2 5.1 %collective-permute-done.4.piece = bf16[256,1024]{1,0:T(8,128)(2,1)S(1)} collective-permute-done((bf16[256,1024]{1,0:T(8,128)(2,1)S(1)}, bf16[256,1024]{1,0:T(8,128)(2,1)S(1)}, u32[]{:S(2)}, u32[]{:S(2)}) %collective-permute-start.4) | collective-permute-done | bytes 524320 | tf_op jit(solution)/shard_map/ppermute | solution.py:43
  26.3 0.2 collective-permute-start.5
  26.5 0.7 %convert_convert_fusion = f32[9,9]{1,0:T(8,128)S(1)} fusion(f32[9,9]{1,0:T(8,128)} %param.19), kind=kLoop, calls=%fused_computation.6 | loop fusion | flops 162 | bytes 648 | tf_op jit(solution)/shard_map/convert_element_type | solution.py:515
  27.2 0.1 slice.33
  27.3 0.1 slice.27
  27.4 0.1 slice.25
  27.4 0.1 slice.35
  27.5 0.1 slice.31
  27.6 0.1 slice.29
  27.6 0.1 pad.4.clone
  27.7 0.1 pad.1.clone
  27.8 0.1 pad_maximum_fusion.1.psf_taps
  27.9 0.1 pad_maximum_fusion.model_taps
  28.0 0.0 copy-start.1
  28.0 1.2 %copy-done.1 = f32[256,1024]{1,0:T(8,128)S(1)} copy-done((f32[256,1024]{1,0:T(8,128)S(1)}, f32[256,1024]{1,0:T(8,128)}, u32[]{:S(2)}) %copy-start.1) | copy-done | bytes 1048600
  29.2 0.0 copy-start.2
  29.2 1.0 %copy-done.2 = bf16[256,1024]{1,0:T(8,128)(2,1)S(1)} copy-done((bf16[256,1024]{1,0:T(8,128)(2,1)S(1)}, bf16[256,1024]{1,0:T(8,128)(2,1)}, u32[]{:S(2)}) %copy-start.2) | copy-done | bytes 524312
  30.2 0.0 copy-start.3
  30.2 0.7 %copy-done.3 = s32[1,4]{1,0:T(1,128)S(1)} copy-done((s32[1,4]{1,0:T(1,128)S(1)}, s32[1,4]{1,0:T(1,128)}, u32[]{:S(2)}) %copy-start.3) | copy-done | bytes 40
  30.9 0.0 copy-start.4
  30.9 0.7 %copy-done.4 = s32[16]{0:T(128)S(1)} copy-done((s32[16]{0:T(128)S(1)}, s32[16]{0:T(128)}, u32[]{:S(2)}) %copy-start.4) | copy-done | bytes 88
  31.6 0.0 copy-start.5
  31.6 0.7 %copy-done.5 = s32[1,4]{1,0:T(1,128)S(1)} copy-done((s32[1,4]{1,0:T(1,128)S(1)}, s32[1,4]{1,0:T(1,128)}, u32[]{:S(2)}) %copy-start.5) | copy-done | bytes 40
  32.2 0.0 copy-start.6
  32.2 0.7 %copy-done.6 = s32[1,4]{1,0:T(1,128)S(1)} copy-done((s32[1,4]{1,0:T(1,128)S(1)}, s32[1,4]{1,0:T(1,128)}, u32[]{:S(2)}) %copy-start.6) | copy-done | bytes 40
  32.9 2.2 %prepare.1 = (s32[1,15]{1,0:T(1,128)S(1)}, bf16[2,12,256,256]{3,2,1,0:T(8,128)(2,1)S(1)}, bf16[2,6,256,256]{3,2,1,0:T(8,128)(2,1)S(1)}, bf16[8,8,128]{2,1,0:T(8,...) custom-call(s32[1,4]{1,0:T(1,128)S(1)} %copy-done.3, ...), custom_call_target="tpu_custom_call" | custom-call | bytes 4194304 | tf_op jit(solution)/shard_map/prepare/pallas_call | solution.py:522
  35.1 0.0 collective-permute-done.refs_0_
  35.1 0.0 collective-permute-done.2.refs_2_
  35.1 4.6 %near.1 = (f32[256,8,128]{2,1,0:T(8,128)S(1)}, f32[256,8,128]{2,1,0:T(8,128)S(1)}) custom-call(s32[1,15]{1,0:T(1,128)S(1)} %get-tuple-element.21.table, f32[2048,128]{1,0:T(8,128)S(1)} %get-tuple-element.22.own, bf16[256,1024]{1,0:T(8,128)(2,1)S(1)} %collective-permute-done.refs_0_, bf16[256,1024]{1,0:T(8,128)(2,1)S(1)} %collective-permute-done.1.refs_1_.pair, ...), custom_call_target="tpu_custom_call" | custom-call | bytes 11534336 | tf_op jit(solution)/shard_map/near/pallas_call | solution.py:555
  39.7 0.7 %relayed.1.partial = f32[256,8,128]{2,1,0:T(8,128)S(1)} custom-call(s32[1,15]{1,0:T(1,128)S(1)} %get-tuple-element.21.table, f32[256,8,128]{2,1,0:T(8,128)S(1)} %get-tuple-element.23.partial, bf16[256,1024]{1,0:T(8,128)(2,1)S(1)} %collective-permute-done.4.piece), custom_call_target="tpu_custom_call" | custom-call | bytes 5242880 | tf_op jit(solution)/shard_map/relayed/pallas_call | solution.py:567
  40.4 0.0 collective-permute-done.5.piece
  40.4 0.8 %canvas.1 = (f32[2048,128]{1,0:T(8,128)S(1)}, bf16[22,8,128]{2,1,0:T(8,128)(2,1)S(1)}, bf16[22,8,128]{2,1,0:T(8,128)(2,1)S(1)}) custom-call(s32[1,15]{1,0:T(1,128)S(1)} %get-tuple-element.21.table, f32[256,8,128]{2,1,0:T(8,128)S(1)} %relayed.1.partial, bf16[256,1024]{1,0:T(8,128)(2,1)S(1)} %collective-permute-done.5.piece, ...), custom_call_target="tpu_custom_call" | custom-call | bytes 5242880 | tf_op jit(solution)/shard_map/canvas/pallas_call | solution.py:577
  41.3 1.9 %collective-permute-start.6 = (bf16[22,8,128]{2,1,0:T(8,128)(2,1)S(1)}, bf16[22,8,128]{2,1,0:T(8,128)(2,1)S(1)}, u32[]{:S(2)}, u32[]{:S(2)}) collective-permute-start(bf16[22,8,128]{2,1,0:T(8,128)(2,1)S(1)} %get-tuple-element.28), channel_id=1, source_target_pairs={{0,1},{1,0},{4,5},{5,4},{8,9},{9,8},{12,13},{13,12},{16,17},{17,16... | collective-permute-start | bytes 135176 | tf_op jit(solution)/shard_map/ppermute | solution.py:591
  43.2 3.2 %collective-permute-start.7 = (bf16[22,8,128]{2,1,0:T(8,128)(2,1)S(1)}, bf16[22,8,128]{2,1,0:T(8,128)(2,1)S(1)}, u32[]{:S(2)}, u32[]{:S(2)}) collective-permute-start(bf16[22,8,128]{2,1,0:T(8,128)(2,1)S(1)} %get-tuple-element.29), channel_id=1, source_target_pairs={{15,0},{0,15},{1,2},{2,1},{3,4},{4,3},{5,6},{6,5},{7,8},{8,7},{9,1... | collective-permute-start | bytes 135176 | tf_op jit(solution)/shard_map/ppermute | solution.py:591
  46.4 1.9 %interior.1 = (f32[2048,128]{1,0:T(8,128)S(1)}, f32[8,128]{1,0:T(8,128)S(1)}) custom-call(f32[2048,128]{1,0:T(8,128)S(1)} %get-tuple-element.27.refs_0_, f32[2048,128]{1,0:T(8,128)S(1)} %get-tuple-element.30.refs_1_.refs_3_, bf16[2,12,256,256]{3,2,1,0:T(8,128)(2,1)S(1)} %get-tuple-element.31.refs_2_.refs_4_), custom_call_target="tpu_custom_call" | custom-call | bytes 7340032 | tf_op jit(solution)/shard_map/interior/pallas_call | solution.py:597
  48.3 0.0 collective-permute-done.6.refs_1_
  48.4 1.1 %collective-permute-done.7.refs_2_ = bf16[22,8,128]{2,1,0:T(8,128)(2,1)S(1)} collective-permute-done((bf16[22,8,128]{2,1,0:T(8,128)(2,1)S(1)}, bf16[22,8,128]{2,1,0:T(8,128)(2,1)S(1)}, u32[]{:S(2)}, u32[]{:S(2)}) %collective-permute-start.7) | collective-permute-done | bytes 45088 | tf_op jit(solution)/shard_map/ppermute | solution.py:591
  49.4 0.9 %edge.1 = (f32[128,128]{1,0:T(8,128)S(1)}, f32[128,128]{1,0:T(8,128)S(1)}, f32[8,128]{1,0:T(8,128)S(1)}) custom-call(f32[2048,128]{1,0:T(8,128)S(1)} %get-tuple-element.27.refs_0_, bf16[22,8,128]{2,1,0:T(8,128)(2,1)S(1)} %collective-permute-done.6.refs_1_, bf16[22,8,128]{2,1,0:T(8,128)(2,1)S(1)} %collective-permute-done.7.refs_2_, ...), custom_call_target="tpu_custom_call" | custom-call | bytes 4194304 | tf_op jit(solution)/shard_map/edge/pallas_call | solution.py:608
  50.4 0.1 collective-permute-start.10
  50.5 3.7 %collective-permute-start.8 = (f32[8,128]{1,0:T(8,128)S(1)}, f32[8,128]{1,0:T(8,128)S(1)}, u32[]{:S(2)}, u32[]{:S(2)}) collective-permute-start(f32[8,128]{1,0:T(8,128)S(1)} %get-tuple-element.39.refs_1_), channel_id=1, source_target_pairs={{15,1},{1,15},{0,2},{2,0},{3,5},{5,3},{4,6},{6,4},{7,9},{9,7},{8,1... | collective-permute-start | bytes 12296 | tf_op jit(solution)/shard_map/ppermute | solution.py:628
  54.2 0.8 %collective-permute-start.9 = (f32[8,128]{1,0:T(8,128)S(1)}, f32[8,128]{1,0:T(8,128)S(1)}, u32[]{:S(2)}, u32[]{:S(2)}) collective-permute-start(f32[8,128]{1,0:T(8,128)S(1)} %get-tuple-element.39.refs_1_), channel_id=1, source_target_pairs={{15,0},{0,15},{1,2},{2,1},{3,4},{4,3},{5,6},{6,5},{7,8},{8,7},{9,1... | collective-permute-start | bytes 12296 | tf_op jit(solution)/shard_map/ppermute | solution.py:628
  55.0 1.9 %rest.1 = (f32[256,1024]{1,0:T(8,128)}, f32[2048,128]{1,0:T(8,128)S(1)}) custom-call(f32[128,128]{1,0:T(8,128)S(1)} %get-tuple-element.33.refs_0_, f32[128,128]{1,0:T(8,128)S(1)} %get-tuple-element.34.refs_1_, f32[2048,128]{1,0:T(8,128)S(1)} %get-tuple-element.35.refs_2_, bf16[2,6,256,256]{3,2,1,0:T(8,128)(2,1)S(1)} %get-tuple-element.36.refs_3_), custom_call_target="tpu_custom_call" | custom-call | bytes 8388608 | tf_op jit(solution)/shard_map/rest/pallas_call | solution.py:630
  56.9 0.0 collective-permute-done.10.refs_4_
  56.9 0.0 collective-permute-done.8.refs_2_
  56.9 3.0 %collective-permute-done.9.refs_3_ = f32[8,128]{1,0:T(8,128)S(1)} collective-permute-done((f32[8,128]{1,0:T(8,128)S(1)}, f32[8,128]{1,0:T(8,128)S(1)}, u32[]{:S(2)}, u32[]{:S(2)}) %collective-permute-start.9) | collective-permute-done | bytes 4128 | tf_op jit(solution)/shard_map/ppermute | solution.py:628
  59.9 1.1 %detection.1 = f32[256,1024]{1,0:T(8,128)} custom-call(f32[2048,128]{1,0:T(8,128)S(1)} %get-tuple-element.38.refs_0_, f32[8,128]{1,0:T(8,128)S(1)} %get-tuple-element.39.refs_1_, f32[8,128]{1,0:T(8,128)S(1)} %collective-permute-done.8.refs_2_, f32[8,128]{1,0:T(8,128)S(1)} %collective-permute-done.9.refs_3_, f32[8,128]{1,0:T(8,128)S(1)} %collective-permute-done.10.refs_4_), custom_call_target="tpu_custom_call" | custom-call | bytes 4194304 | tf_op jit(solution)/shard_map/detection/pallas_call | solution.py:644
  (4 shorter events, 0.0 us)
Async XLA Ops:
  0.6 19.1 %copy-start = (f32[4,20]{1,0:T(4,128)S(1)}, f32[4,20]{1,0:T(4,128)}, u32[]{:S(2)}) copy-start(f32[4,20]{1,0:T(4,128)} %param.18) | copy-start | bytes 964
  0.6 15.2 %collective-permute-start.1 = (bf16[256,1024]{1,0:T(8,128)(2,1)}, bf16[256,1024]{1,0:T(8,128)(2,1)S(1)}, u32[]{:S(2)}, u32[]{:S(2)}) collective-permute-start(bf16[256,1024]{1,0:T(8,128)(2,1)} %piece_in.1), channel_id=1, source_target_pairs={{0,2},{1,3},{2,0},{3,1},{4,6},{5,7},{6,4},{7,5},{8,10},{9,11},{10,... | collective-permute-start | bytes 1572872 | tf_op jit(solution)/shard_map/ppermute | solution.py:43
  3.7 12.1 %collective-permute-start.3 = (bf16[256,1024]{1,0:T(8,128)(2,1)}, bf16[256,1024]{1,0:T(8,128)(2,1)S(1)}, u32[]{:S(2)}, u32[]{:S(2)}) collective-permute-start(bf16[256,1024]{1,0:T(8,128)(2,1)} %piece_in.1), channel_id=1, source_target_pairs={{1,4},{3,6},{4,1},{5,8},{6,3},{7,10},{8,5},{9,12},{10,7},{11,14},{... | collective-permute-start | bytes 1572872 | tf_op jit(solution)/shard_map/ppermute | solution.py:43
  15.9 10.4 %collective-permute-start.4 = (bf16[256,1024]{1,0:T(8,128)(2,1)S(1)}, bf16[256,1024]{1,0:T(8,128)(2,1)S(1)}, u32[]{:S(2)}, u32[]{:S(2)}) collective-permute-start(bf16[256,1024]{1,0:T(8,128)(2,1)S(1)} %relay.1), channel_id=1, source_target_pairs={{0,4},{1,2},{2,1},{4,8},{5,6},{6,5},{7,3},{8,12},{9,10},{10,9},{11... | collective-permute-start | bytes 1572872 | tf_op jit(solution)/shard_map/ppermute | solution.py:43
  19.6 15.5 %collective-permute-start = (bf16[256,1024]{1,0:T(8,128)(2,1)}, bf16[256,1024]{1,0:T(8,128)(2,1)S(1)}, u32[]{:S(2)}, u32[]{:S(2)}) collective-permute-start(bf16[256,1024]{1,0:T(8,128)(2,1)} %piece_in.1), channel_id=1, source_target_pairs={{0,1},{1,0},{2,3},{3,2},{4,5},{5,4},{6,7},{7,6},{8,9},{9,8},{10,11... | collective-permute-start | bytes 1572872 | tf_op jit(solution)/shard_map/ppermute | solution.py:43
  20.7 14.4 %collective-permute-start.2 = (bf16[256,1024]{1,0:T(8,128)(2,1)S(1)}, bf16[256,1024]{1,0:T(8,128)(2,1)S(1)}, u32[]{:S(2)}, u32[]{:S(2)}) collective-permute-start(bf16[256,1024]{1,0:T(8,128)(2,1)S(1)} %collective-permute-done.1.refs_1_.pair), channel_id=1, source_target_pairs={{0,1},{1,0},{2,3},{3,2},{4,5},{5,4},{6,7},{7,6},{8,9},{9,8},{10,11... | collective-permute-start | bytes 1572872 | tf_op jit(solution)/shard_map/ppermute | solution.py:43
  26.3 14.1 %collective-permute-start.5 = (bf16[256,1024]{1,0:T(8,128)(2,1)S(1)}, bf16[256,1024]{1,0:T(8,128)(2,1)S(1)}, u32[]{:S(2)}, u32[]{:S(2)}) collective-permute-start(bf16[256,1024]{1,0:T(8,128)(2,1)S(1)} %collective-permute-done.4.piece), channel_id=1, source_target_pairs={{0,1},{1,0},{2,3},{3,2},{4,5},{5,4},{6,7},{7,6},{8,9},{9,8},{10,11... | collective-permute-start | bytes 1572872 | tf_op jit(solution)/shard_map/ppermute | solution.py:43
  28.0 1.2 %copy-start.1 = (f32[256,1024]{1,0:T(8,128)S(1)}, f32[256,1024]{1,0:T(8,128)}, u32[]{:S(2)}) copy-start(f32[256,1024]{1,0:T(8,128)} %science_in.1) | copy-start | bytes 3145732
  29.2 1.0 %copy-start.2 = (bf16[256,1024]{1,0:T(8,128)(2,1)S(1)}, bf16[256,1024]{1,0:T(8,128)(2,1)}, u32[]{:S(2)}) copy-start(bf16[256,1024]{1,0:T(8,128)(2,1)} %piece_in.1) | copy-start | bytes 1572868
  30.2 0.7 %copy-start.3 = (s32[1,4]{1,0:T(1,128)S(1)}, s32[1,4]{1,0:T(1,128)}, u32[]{:S(2)}) copy-start(s32[1,4]{1,0:T(1,128)} %covering_in.1) | copy-start | bytes 52
  30.9 0.7 %copy-start.4 = (s32[16]{0:T(128)S(1)}, s32[16]{0:T(128)}, u32[]{:S(2)}) copy-start(s32[16]{0:T(128)} %owner_in.1) | copy-start | bytes 196
  31.6 0.7 %copy-start.5 = (s32[1,4]{1,0:T(1,128)S(1)}, s32[1,4]{1,0:T(1,128)}, u32[]{:S(2)}) copy-start(s32[1,4]{1,0:T(1,128)} %row_in.1) | copy-start | bytes 52
  32.2 0.7 %copy-start.6 = (s32[1,4]{1,0:T(1,128)S(1)}, s32[1,4]{1,0:T(1,128)}, u32[]{:S(2)}) copy-start(s32[1,4]{1,0:T(1,128)} %col_in.1) | copy-start | bytes 52
  41.3 7.1 %collective-permute-start.6 = (bf16[22,8,128]{2,1,0:T(8,128)(2,1)S(1)}, bf16[22,8,128]{2,1,0:T(8,128)(2,1)S(1)}, u32[]{:S(2)}, u32[]{:S(2)}) collective-permute-start(bf16[22,8,128]{2,1,0:T(8,128)(2,1)S(1)} %get-tuple-element.28), channel_id=1, source_target_pairs={{0,1},{1,0},{4,5},{5,4},{8,9},{9,8},{12,13},{13,12},{16,17},{17,16... | collective-permute-start | bytes 135176 | tf_op jit(solution)/shard_map/ppermute | solution.py:591
  43.2 6.2 %collective-permute-start.7 = (bf16[22,8,128]{2,1,0:T(8,128)(2,1)S(1)}, bf16[22,8,128]{2,1,0:T(8,128)(2,1)S(1)}, u32[]{:S(2)}, u32[]{:S(2)}) collective-permute-start(bf16[22,8,128]{2,1,0:T(8,128)(2,1)S(1)} %get-tuple-element.29), channel_id=1, source_target_pairs={{15,0},{0,15},{1,2},{2,1},{3,4},{4,3},{5,6},{6,5},{7,8},{8,7},{9,1... | collective-permute-start | bytes 135176 | tf_op jit(solution)/shard_map/ppermute | solution.py:591
  50.4 6.5 %collective-permute-start.10 = (f32[8,128]{1,0:T(8,128)S(1)}, f32[8,128]{1,0:T(8,128)S(1)}, u32[]{:S(2)}, u32[]{:S(2)}) collective-permute-start(f32[8,128]{1,0:T(8,128)S(1)} %get-tuple-element.39.refs_1_), channel_id=1, source_target_pairs={{15,2},{2,15},{0,1},{1,0},{3,6},{6,3},{4,5},{5,4},{7,10},{10,7},{8... | collective-permute-start | bytes 12296 | tf_op jit(solution)/shard_map/ppermute | solution.py:628
  50.5 6.4 %collective-permute-start.8 = (f32[8,128]{1,0:T(8,128)S(1)}, f32[8,128]{1,0:T(8,128)S(1)}, u32[]{:S(2)}, u32[]{:S(2)}) collective-permute-start(f32[8,128]{1,0:T(8,128)S(1)} %get-tuple-element.39.refs_1_), channel_id=1, source_target_pairs={{15,1},{1,15},{0,2},{2,0},{3,5},{5,3},{4,6},{6,4},{7,9},{9,7},{8,1... | collective-permute-start | bytes 12296 | tf_op jit(solution)/shard_map/ppermute | solution.py:628
  54.2 5.7 %collective-permute-start.9 = (f32[8,128]{1,0:T(8,128)S(1)}, f32[8,128]{1,0:T(8,128)S(1)}, u32[]{:S(2)}, u32[]{:S(2)}) collective-permute-start(f32[8,128]{1,0:T(8,128)S(1)} %get-tuple-element.39.refs_1_), channel_id=1, source_target_pairs={{15,0},{0,15},{1,2},{2,1},{3,4},{4,3},{5,6},{6,5},{7,8},{8,7},{9,1... | collective-permute-start | bytes 12296 | tf_op jit(solution)/shard_map/ppermute | solution.py:628
